TPU v7x, 32 devices: a whole 2x2x4 slice. The times are simulated.
32 devices in a mesh: seg: 4 (over y, x), sec: 8 (over z, core).
Axes of the slice: x: 2, y: 2, z: 4, core: 2. Of those that a mesh axis runs over, the one named last changes fastest.
Arguments:
- psi: float32 [4, 8, 256, 256], P('seg', 'sec'), may hold values from -17 to 17
- sector_dims: int32 [4, 8, 2], P('seg', 'sec'), may hold values from 64 to 256, as said below
- env_left: bfloat16 [4, 8, 30, 256, 256], P('seg', 'sec'), may hold values from -2 to 5
- env_right: bfloat16 [4, 8, 30, 256, 256], P('seg', 'sec'), may hold values from -2 to 5
Outputs:
- second_vector: float32 [4, 8, 256, 256], P('seg', 'sec')
- third_vector: float32 [4, 8, 256, 256], P('seg', 'sec')
- last_image: float32 [4, 8, 256, 256], P('seg', 'sec')
- coefficients: float32 [4, 5], P('seg')
- boundary: float32 [4, 8, 256, 256], P('seg', 'sec')
Inputs may be any that keep to these rules, and one draw needn't show every extreme that they name: `sector_dims`: the largest live dimension of every segment is 256.
All inputs are finite; a program needn't handle non-finite values.
Results may differ from a plain program's by a relative error of at most 0.0095.
Values may be sent and summed in bfloat16 or wider, within the bound.
No kernel may reach another device: no remote copies, remote signals or barrier semaphores. Data moves between devices by JAX's collectives and lax.ppermute only.
A program may use at most 64 MiB of HBM per device.

v0:
```python
import jax
import jax.numpy as jnp
from jax import lax
from jax.sharding import PartitionSpec as P

W_ZERO = 6
W_HOP = 6
GRID = 4


EPSILON = 1e-06


def shifted(block, axis, distance):
    devices = range(lax.axis_size(axis))
    route = [(i - distance, i) for i in devices if i - distance in devices]
    return lax.ppermute(block, axis, route)


def body(psi, sector_dims, env_left, env_right):
    size = psi.shape[-1]
    count = lax.axis_size("sec")
    entries = jnp.float32(count * size * size)
    index = lax.axis_index("sec")
    column = index % GRID
    row_pos = index // GRID
    rows = lax.broadcasted_iota(jnp.int32, (size, size), 0)
    cols = lax.broadcasted_iota(jnp.int32, (size, size), 1)
    mask = ((rows < sector_dims[0, 0, 0]) & (cols < sector_dims[0, 0, 1])).astype(jnp.float32)
    left_env = env_left[0, 0]
    right_env = env_right[0, 0]
    flags = [column >= 1, column <= GRID - 2, row_pos >= 1, row_pos <= count // GRID - 2]
    offsets = (1, -1, GRID, -GRID)

    def neighbours(low):
        found = []
        for offset in offsets:
            found.append(shifted(low, "sec", offset))
        return [jnp.where(flag, block, jnp.zeros_like(block)) for flag, block in zip(flags, found)]

    def contract(block, start, stop):
        inner = jnp.einsum(
            "wij,jk->wik", left_env[start:stop], block, preferred_element_type=jnp.float32
        ).astype(jnp.bfloat16)
        return jnp.einsum(
            "wik,wlk->il", inner, right_env[start:stop], preferred_element_type=jnp.float32
        )

    start_vec = psi[0, 0] * mask
    squared_start = lax.psum(jnp.sum(start_vec * start_vec), "sec")
    current = start_vec / jnp.sqrt(squared_start / entries + EPSILON)
    previous = jnp.zeros_like(current)
    beta = jnp.float32(0.0)
    alphas = []
    betas = []
    vectors = []
    image = current
    for step in range(3):
        apply_low = current.astype(jnp.bfloat16)
        total = contract(apply_low, 0, W_ZERO)
        for group, apply_block in enumerate(neighbours(apply_low)):
            apply_start = W_ZERO + group * W_HOP
            total = total + contract(apply_block, apply_start, apply_start + W_HOP)
        image = total * mask
        moments = lax.psum(
            (
                jnp.sum(image * image),
                jnp.sum(image * current),
                jnp.sum(image * previous),
                jnp.sum(current * current),
                jnp.sum(previous * previous),
                jnp.sum(current * previous),
            ),
            "sec",
        )
        img_img, img_cur, img_prev, cur_cur, prev_prev, cur_prev = moments
        alpha = img_cur / entries
        if step < 2:
            squared = (
                img_img
                + alpha * alpha * cur_cur
                + beta * beta * prev_prev
                - 2.0 * alpha * img_cur
                - 2.0 * beta * img_prev
                + 2.0 * alpha * beta * cur_prev
            )
            residual = image - alpha * current - beta * previous
            beta_next = jnp.sqrt(squared / entries + EPSILON)
        alphas.append(alpha)
        if step < 2:
            betas.append(beta_next)
            previous = current
            current = residual / beta_next
            beta = beta_next
            vectors.append(current)
    own = vectors[1].astype(jnp.bfloat16)
    before = shifted(own, "seg", 1)
    envpart = jnp.dot(left_env[0], own, preferred_element_type=jnp.float32).astype(jnp.bfloat16)
    boundary = (
        jnp.dot(own.T, envpart, preferred_element_type=jnp.float32)
        + jnp.dot(before.T, envpart, preferred_element_type=jnp.float32)
    ) / jnp.sqrt(jnp.float32(size))
    coeffs = jnp.stack([alphas[0], alphas[1], alphas[2], betas[0], betas[1]])
    return (
        vectors[0][None, None],
        vectors[1][None, None],
        image[None, None],
        coeffs[None],
        boundary[None, None],
    )


def solution(mesh):
    in_specs = (
        P("seg", "sec", None, None),
        P("seg", "sec", None),
        P("seg", "sec", None, None, None),
        P("seg", "sec", None, None, None),
    )
    out_specs = (
        P("seg", "sec", None, None),
        P("seg", "sec", None, None),
        P("seg", "sec", None, None),
        P("seg", None),
        P("seg", "sec", None, None),
    )
    return jax.shard_map(body, mesh=mesh, in_specs=in_specs, out_specs=out_specs, check_vma=False)
```

profile of v0, /device:TPU:0, one launch (start us, length us, event | category | flops | bytes accessed | tf_op | source)
XLA Modules:
  0.0 159.4 jit_solution(1309333121906924811)
XLA Ops:
  0.6 1.3 fusion.293
  1.9 1.3 iota_compare_fusion
  3.2 1.7 %multiply_reduce_fusion.11 = f32[]{:T(128)} fusion(f32[1,1,256,256]{3,2,1,0:T(8,128)} %param.4, pred[256]{0:T(512)(128)(4,1)S(1)} %get-tuple-element.38, pred[256]{0:T(512)(128)(4,1)S(1)} %get-tuple-element.39), kind=kLoop, calls=%fused_computation.154 | loop fusion | flops 262143 | bytes 262660 | tf_op jit(solution)/shard_map/reduce_sum | solution.py:50
  4.9 18.7 %psum.94 = f32[]{:T(128)} all-reduce(f32[]{:T(128)} %multiply_reduce_fusion.11), channel_id=1, replica_groups=mesh['seg'=4,'sec'=8] {'sec'}, use_global_device_ids=true, to_apply=%region_1.2 | all-reduce | flops 1 | bytes 8 | tf_op jit(solution)/shard_map/psum | solution.py:50
  24.4 1.1 fusion.291
  25.4 1.3 collective-permute-start.3
  26.7 5.5 %collective-permute-start.2 = (bf16[256,256]{1,0:T(8,128)(2,1)S(1)}, bf16[256,256]{1,0:T(8,128)(2,1)S(1)}, u32[]{:S(2)}, u32[]{:S(2)}) collective-permute-start(bf16[256,256]{1,0:T(8,128)(2,1)S(1)} %get-tuple-element.30), channel_id=1, source_target_pairs={{0,4},{1,5},{2,6},{3,7},{8,12},{9,13},{10,14},{11,15},{16,20},{17,... | collective-permute-start | bytes 393224 | tf_op jit(solution)/shard_map/ppermute | solution.py:17
  32.2 1.3 collective-permute-start.1
  33.5 3.0 %collective-permute-start = (bf16[256,256]{1,0:T(8,128)(2,1)S(1)}, bf16[256,256]{1,0:T(8,128)(2,1)S(1)}, u32[]{:S(2)}, u32[]{:S(2)}) collective-permute-start(bf16[256,256]{1,0:T(8,128)(2,1)S(1)} %get-tuple-element.30), channel_id=1, source_target_pairs={{0,1},{1,2},{2,3},{3,4},{4,5},{5,6},{6,7},{8,9},{9,10},{10,11},{11... | collective-permute-start | bytes 393224 | tf_op jit(solution)/shard_map/ppermute | solution.py:17
  36.6 2.4 %fusion.46 = f32[256,256]{1,0:T(8,128)S(1)} fusion(bf16[1,1,30,256,256]{4,3,2,1,0:T(8,128)(2,1)} %param.7, bf16[1,1,30,256,256]{4,3,2,1,0:T(8,128)(2,1)} %param.6, f32[1,1,256,256]{3,2,1,0:T(8,128)} %param.4, f32[]{:T(128)S(6)} %sqrt.9, pred[256]{0:T(512)(128)(4,1)S(1)} %get-tuple-element.38, pred[256]{0:T(512)(128)(4,1)S(1)} %get-tuple-element.39), kind=kOutput, calls=%fused_computation.62 | convolution fusion | flops 403308544 | bytes 2097668 | tf_op jit(solution)/shard_map/wik,wlk->il/dot_general | solution.py:45
  38.9 0.0 collective-permute-done.3
  38.9 2.2 %fusion.42 = f32[256,256]{1,0:T(8,128)S(1)} fusion(bf16[1,1,30,256,256]{4,3,2,1,0:T(8,128)(2,1)} %param.7, bf16[1,1,30,256,256]{4,3,2,1,0:T(8,128)(2,1)} %param.6, bf16[256,256]{1,0:T(8,128)(2,1)S(1)} %collective-permute-done.3, pred[]{:T(512)S(6)} %le.7), kind=kOutput, calls=%fused_computation.58 | convolution fusion | flops 403111936 | bytes 1966081 | tf_op jit(solution)/shard_map/wik,wlk->il/dot_general | solution.py:45
  41.1 0.0 collective-permute-done.2
  41.1 2.2 %fusion.43 = f32[256,256]{1,0:T(8,128)S(1)} fusion(bf16[1,1,30,256,256]{4,3,2,1,0:T(8,128)(2,1)} %param.7, bf16[1,1,30,256,256]{4,3,2,1,0:T(8,128)(2,1)} %param.6, bf16[256,256]{1,0:T(8,128)(2,1)S(1)} %collective-permute-done.2, pred[]{:T(512)S(6)} %ge.7), kind=kOutput, calls=%fused_computation.59 | convolution fusion | flops 403111936 | bytes 1966081 | tf_op jit(solution)/shard_map/wik,wlk->il/dot_general | solution.py:45
  43.3 0.0 collective-permute-done.1
  43.4 2.2 %fusion.44 = f32[256,256]{1,0:T(8,128)S(1)} fusion(bf16[1,1,30,256,256]{4,3,2,1,0:T(8,128)(2,1)} %param.7, bf16[1,1,30,256,256]{4,3,2,1,0:T(8,128)(2,1)} %param.6, bf16[256,256]{1,0:T(8,128)(2,1)S(1)} %collective-permute-done.1, pred[]{:T(512)S(6)} %le.6), kind=kOutput, calls=%fused_computation.60 | convolution fusion | flops 403111936 | bytes 1966081 | tf_op jit(solution)/shard_map/wik,wlk->il/dot_general | solution.py:45
  45.6 0.0 collective-permute-done
  45.6 2.9 %multiply_reduce_fusion.6 = (f32[]{:T(128)}, f32[]{:T(128)}, f32[]{:T(128)}, f32[]{:T(128)}, f32[]{:T(128)}, /*index=5*/f32[256,256]{1,0:T(8,128)S(1)}) fusion(f32[256,256]{1,0:T(8,128)S(1)} %get-tuple-element.31, f32[256,256]{1,0:T(8,128)S(1)} %fusion.42, f32[256,256]{1,0:T(8,128)S(1)} %fusion.43, f32[256,256]{1,0:T(8,128)S(1)} %fusion.44, ...), kind=kOutput, calls=%fused_computation.147 | convolution fusion | flops 404160512 | bytes 3277333 | tf_op jit(solution)/shard_map/wik,wlk->il/dot_general | solution.py:45
  48.4 14.8 %all-reduce.1 = (f32[]{:T(128)}, f32[]{:T(128)}, f32[]{:T(128)}, f32[]{:T(128)}, f32[]{:T(128)}, /*index=5*/f32[]{:T(128)}) all-reduce(f32[]{:T(128)} %get-tuple-element.14, f32[]{:T(128)} %get-tuple-element.12, f32[]{:T(128)} %get-tuple-element.11, f32[]{:T(128)} %constant.51.clone.1, ...), channel_id=1, replica_groups=mesh['seg'=4,'sec'=8] {'sec'}, use_global_device_ids=true, to_apply=%region_5.6 | all-reduce | flops 6 | bytes 48 | tf_op jit(solution)/shard_map/psum | solution.py:65
  70.4 0.0 copy-start
  70.4 1.3 collective-permute-start.7
  71.7 5.5 %collective-permute-start.6 = (bf16[256,256]{1,0:T(8,128)(2,1)S(1)}, bf16[256,256]{1,0:T(8,128)(2,1)S(1)}, u32[]{:S(2)}, u32[]{:S(2)}) collective-permute-start(bf16[256,256]{1,0:T(8,128)(2,1)S(1)} %get-tuple-element.28), channel_id=1, source_target_pairs={{0,4},{1,5},{2,6},{3,7},{8,12},{9,13},{10,14},{11,15},{16,20},{17,... | collective-permute-start | bytes 393224 | tf_op jit(solution)/shard_map/ppermute | solution.py:17
  77.2 1.3 collective-permute-start.5
  78.5 3.0 %collective-permute-start.4 = (bf16[256,256]{1,0:T(8,128)(2,1)S(1)}, bf16[256,256]{1,0:T(8,128)(2,1)S(1)}, u32[]{:S(2)}, u32[]{:S(2)}) collective-permute-start(bf16[256,256]{1,0:T(8,128)(2,1)S(1)} %get-tuple-element.28), channel_id=1, source_target_pairs={{0,1},{1,2},{2,3},{3,4},{4,5},{5,6},{6,7},{8,9},{9,10},{10,11},{11... | collective-permute-start | bytes 393224 | tf_op jit(solution)/shard_map/ppermute | solution.py:17
  82.2 2.2 %fusion.41 = f32[256,256]{1,0:T(8,128)S(1)} fusion(bf16[1,1,30,256,256]{4,3,2,1,0:T(8,128)(2,1)} %param.7, bf16[1,1,30,256,256]{4,3,2,1,0:T(8,128)(2,1)} %param.6, bf16[256,256]{1,0:T(8,128)(2,1)S(1)} %get-tuple-element.28), kind=kOutput, calls=%fused_computation.57 | convolution fusion | flops 403046400 | bytes 1966080 | tf_op jit(solution)/shard_map/wik,wlk->il/dot_general | solution.py:45
  84.4 0.0 collective-permute-done.7
  84.4 2.2 %fusion.37 = f32[256,256]{1,0:T(8,128)S(1)} fusion(bf16[1,1,30,256,256]{4,3,2,1,0:T(8,128)(2,1)} %param.7, bf16[1,1,30,256,256]{4,3,2,1,0:T(8,128)(2,1)} %param.6, bf16[256,256]{1,0:T(8,128)(2,1)S(1)} %collective-permute-done.7, pred[]{:T(512)S(6)} %le.7), kind=kOutput, calls=%fused_computation.53 | convolution fusion | flops 403111936 | bytes 1966081 | tf_op jit(solution)/shard_map/wik,wlk->il/dot_general | solution.py:45
  86.6 0.0 collective-permute-done.6
  86.6 2.2 %fusion.38 = f32[256,256]{1,0:T(8,128)S(1)} fusion(bf16[1,1,30,256,256]{4,3,2,1,0:T(8,128)(2,1)} %param.7, bf16[1,1,30,256,256]{4,3,2,1,0:T(8,128)(2,1)} %param.6, bf16[256,256]{1,0:T(8,128)(2,1)S(1)} %collective-permute-done.6, pred[]{:T(512)S(6)} %ge.7), kind=kOutput, calls=%fused_computation.54 | convolution fusion | flops 403111936 | bytes 1966081 | tf_op jit(solution)/shard_map/wik,wlk->il/dot_general | solution.py:45
  88.8 0.0 collective-permute-done.5
  88.8 2.2 %fusion.39 = f32[256,256]{1,0:T(8,128)S(1)} fusion(bf16[1,1,30,256,256]{4,3,2,1,0:T(8,128)(2,1)} %param.7, bf16[1,1,30,256,256]{4,3,2,1,0:T(8,128)(2,1)} %param.6, bf16[256,256]{1,0:T(8,128)(2,1)S(1)} %collective-permute-done.5, pred[]{:T(512)S(6)} %le.6), kind=kOutput, calls=%fused_computation.55 | convolution fusion | flops 403111936 | bytes 1966081 | tf_op jit(solution)/shard_map/wik,wlk->il/dot_general | solution.py:45
  91.0 0.0 collective-permute-done.4
  91.0 2.9 %multiply_reduce_fusion.1 = (f32[]{:T(128)}, f32[]{:T(128)}, f32[]{:T(128)}, f32[]{:T(128)}, f32[]{:T(128)}, /*index=5*/f32[256,256]{1,0:T(8,128)S(1)}) fusion(f32[256,256]{1,0:T(8,128)S(1)} %get-tuple-element.29, f32[256,256]{1,0:T(8,128)S(1)} %get-tuple-element.31, f32[256,256]{1,0:T(8,128)S(1)} %fusion.37, f32[256,256]{1,0:T(8,128)S(1)} %fusion.38, ...), kind=kOutput, calls=%fused_computation.141 | convolution fusion | flops 404160512 | bytes 3539477 | tf_op jit(solution)/shard_map/wik,wlk->il/dot_general | solution.py:45
  93.9 14.8 %all-reduce = (f32[]{:T(128)}, f32[]{:T(128)}, f32[]{:T(128)}, f32[]{:T(128)}, f32[]{:T(128)}) all-reduce(f32[]{:T(128)} %get-tuple-element.8, f32[]{:T(128)} %get-tuple-element.7, f32[]{:T(128)} %get-tuple-element.9, f32[]{:T(128)} %get-tuple-element.6, f32[]{:T(128)} %get-tuple-element.5), channel_id=1, replica_groups=mesh['seg'=4,'sec'=8] {'sec'}, use_global_device_ids=true, to_apply=%region_16.17 | all-reduce | flops 5 | bytes 40 | tf_op jit(solution)/shard_map/psum | solution.py:65
  114.6 0.0 copy-done
  114.6 0.1 fusion.289
  114.7 0.0 copy-start.1
  114.7 1.3 collective-permute-start.11
  116.0 5.5 %collective-permute-start.10 = (bf16[256,256]{1,0:T(8,128)(2,1)S(1)}, bf16[256,256]{1,0:T(8,128)(2,1)S(1)}, u32[]{:S(2)}, u32[]{:S(2)}) collective-permute-start(bf16[256,256]{1,0:T(8,128)(2,1)S(1)} %get-tuple-element.26), channel_id=1, source_target_pairs={{0,4},{1,5},{2,6},{3,7},{8,12},{9,13},{10,14},{11,15},{16,20},{17,... | collective-permute-start | bytes 393224 | tf_op jit(solution)/shard_map/ppermute | solution.py:17
  121.5 1.3 collective-permute-start.9
  122.8 3.0 %collective-permute-start.8 = (bf16[256,256]{1,0:T(8,128)(2,1)S(1)}, bf16[256,256]{1,0:T(8,128)(2,1)S(1)}, u32[]{:S(2)}, u32[]{:S(2)}) collective-permute-start(bf16[256,256]{1,0:T(8,128)(2,1)S(1)} %get-tuple-element.26), channel_id=1, source_target_pairs={{0,1},{1,2},{2,3},{3,4},{4,5},{5,6},{6,7},{8,9},{9,10},{10,11},{11... | collective-permute-start | bytes 393224 | tf_op jit(solution)/shard_map/ppermute | solution.py:17
  125.8 1.1 convolution_convert_fusion.15
  127.0 3.4 %collective-permute-start.12 = (bf16[256,256]{1,0:T(8,128)(2,1)S(1)}, bf16[256,256]{1,0:T(8,128)(2,1)S(1)}, u32[]{:S(2)}, u32[]{:S(2)}) collective-permute-start(bf16[256,256]{1,0:T(8,128)(2,1)S(1)} %get-tuple-element.26), channel_id=1, source_target_pairs={{0,8},{8,16},{16,24},{1,9},{9,17},{17,25},{2,10},{10,18},{18,26},{... | collective-permute-start | bytes 393224 | tf_op jit(solution)/shard_map/ppermute | solution.py:17
  130.4 0.2 fusion.306
  130.6 2.2 %fusion.36 = f32[256,256]{1,0:T(8,128)S(1)} fusion(bf16[1,1,30,256,256]{4,3,2,1,0:T(8,128)(2,1)} %param.7, bf16[1,1,30,256,256]{4,3,2,1,0:T(8,128)(2,1)} %param.6, bf16[256,256]{1,0:T(8,128)(2,1)S(1)} %get-tuple-element.26), kind=kOutput, calls=%fused_computation.52 | convolution fusion | flops 403046400 | bytes 1966080 | tf_op jit(solution)/shard_map/wik,wlk->il/dot_general | solution.py:45
  132.8 0.0 collective-permute-done.11
  132.8 2.2 %fusion.32 = f32[256,256]{1,0:T(8,128)S(1)} fusion(bf16[1,1,30,256,256]{4,3,2,1,0:T(8,128)(2,1)} %param.7, bf16[1,1,30,256,256]{4,3,2,1,0:T(8,128)(2,1)} %param.6, bf16[256,256]{1,0:T(8,128)(2,1)S(1)} %collective-permute-done.11, pred[]{:T(512)S(6)} %le.7), kind=kOutput, calls=%fused_computation.48 | convolution fusion | flops 403111936 | bytes 1966081 | tf_op jit(solution)/shard_map/wik,wlk->il/dot_general | solution.py:45
  135.0 0.0 collective-permute-done.10
  135.0 2.2 %fusion.33 = f32[256,256]{1,0:T(8,128)S(1)} fusion(bf16[1,1,30,256,256]{4,3,2,1,0:T(8,128)(2,1)} %param.7, bf16[1,1,30,256,256]{4,3,2,1,0:T(8,128)(2,1)} %param.6, bf16[256,256]{1,0:T(8,128)(2,1)S(1)} %collective-permute-done.10, pred[]{:T(512)S(6)} %ge.7), kind=kOutput, calls=%fused_computation.49 | convolution fusion | flops 403111936 | bytes 1966081 | tf_op jit(solution)/shard_map/wik,wlk->il/dot_general | solution.py:45
  137.2 0.0 collective-permute-done.9
  137.2 2.2 %fusion.34 = f32[256,256]{1,0:T(8,128)S(1)} fusion(bf16[1,1,30,256,256]{4,3,2,1,0:T(8,128)(2,1)} %param.7, bf16[1,1,30,256,256]{4,3,2,1,0:T(8,128)(2,1)} %param.6, bf16[256,256]{1,0:T(8,128)(2,1)S(1)} %collective-permute-done.9, pred[]{:T(512)S(6)} %le.6), kind=kOutput, calls=%fused_computation.50 | convolution fusion | flops 403111936 | bytes 1966081 | tf_op jit(solution)/shard_map/wik,wlk->il/dot_general | solution.py:45
  139.4 0.0 collective-permute-done.8
  139.4 0.0 copy-done.1
  139.5 3.5 %multiply_reduce_fusion = (f32[]{:T(128)}, f32[256,256]{1,0:T(8,128)}) fusion(f32[256,256]{1,0:T(8,128)S(1)} %get-tuple-element.27, f32[256,256]{1,0:T(8,128)S(1)} %fusion.32, f32[256,256]{1,0:T(8,128)S(1)} %fusion.33, f32[256,256]{1,0:T(8,128)S(1)} %fusion.34, f32[256,256]{1,0:T(8,128)S(1)} %fusion.36, bf16[1,1,30,256,256]{4,3,2,1,0:T(8,128)(2,1)} %param.7, ...), kind=kOutput, calls=%fused_computation.140 | convolution fusion | flops 403636224 | bytes 3277317 | tf_op jit(solution)/shard_map/wik,wlk->il/dot_general | solution.py:45
  143.0 14.2 %psum.106 = f32[]{:T(128)} all-reduce(f32[]{:T(128)} %get-tuple-element.36), channel_id=1, replica_groups=mesh['seg'=4,'sec'=8] {'sec'}, use_global_device_ids=true, to_apply=%region_24.25 | all-reduce | flops 1 | bytes 8 | tf_op jit(solution)/shard_map/psum | solution.py:65
  157.8 0.6 stack.23
  158.4 0.0 collective-permute-done.12
  158.4 0.9 fusion.31
  (1 shorter events, 0.0 us)
Async XLA Ops:
  25.4 13.5 %collective-permute-start.3 = (bf16[256,256]{1,0:T(8,128)(2,1)S(1)}, bf16[256,256]{1,0:T(8,128)(2,1)S(1)}, u32[]{:S(2)}, u32[]{:S(2)}) collective-permute-start(bf16[256,256]{1,0:T(8,128)(2,1)S(1)} %get-tuple-element.30), channel_id=1, source_target_pairs={{4,0},{5,1},{6,2},{7,3},{12,8},{13,9},{14,10},{15,11},{20,16},{21,... | collective-permute-start | bytes 393224 | tf_op jit(solution)/shard_map/ppermute | solution.py:17
  26.7 14.4 %collective-permute-start.2 = (bf16[256,256]{1,0:T(8,128)(2,1)S(1)}, bf16[256,256]{1,0:T(8,128)(2,1)S(1)}, u32[]{:S(2)}, u32[]{:S(2)}) collective-permute-start(bf16[256,256]{1,0:T(8,128)(2,1)S(1)} %get-tuple-element.30), channel_id=1, source_target_pairs={{0,4},{1,5},{2,6},{3,7},{8,12},{9,13},{10,14},{11,15},{16,20},{17,... | collective-permute-start | bytes 393224 | tf_op jit(solution)/shard_map/ppermute | solution.py:17
  32.2 11.2 %collective-permute-start.1 = (bf16[256,256]{1,0:T(8,128)(2,1)S(1)}, bf16[256,256]{1,0:T(8,128)(2,1)S(1)}, u32[]{:S(2)}, u32[]{:S(2)}) collective-permute-start(bf16[256,256]{1,0:T(8,128)(2,1)S(1)} %get-tuple-element.30), channel_id=1, source_target_pairs={{1,0},{2,1},{3,2},{4,3},{5,4},{6,5},{7,6},{9,8},{10,9},{11,10},{12... | collective-permute-start | bytes 393224 | tf_op jit(solution)/shard_map/ppermute | solution.py:17
  33.5 12.1 %collective-permute-start = (bf16[256,256]{1,0:T(8,128)(2,1)S(1)}, bf16[256,256]{1,0:T(8,128)(2,1)S(1)}, u32[]{:S(2)}, u32[]{:S(2)}) collective-permute-start(bf16[256,256]{1,0:T(8,128)(2,1)S(1)} %get-tuple-element.30), channel_id=1, source_target_pairs={{0,1},{1,2},{2,3},{3,4},{4,5},{5,6},{6,7},{8,9},{9,10},{10,11},{11... | collective-permute-start | bytes 393224 | tf_op jit(solution)/shard_map/ppermute | solution.py:17
  70.4 44.2 %copy-start = (f32[256,256]{1,0:T(8,128)}, f32[256,256]{1,0:T(8,128)S(1)}, u32[]{:S(2)}) copy-start(f32[256,256]{1,0:T(8,128)S(1)} %get-tuple-element.29) | copy-start | bytes 786436
  70.4 14.0 %collective-permute-start.7 = (bf16[256,256]{1,0:T(8,128)(2,1)S(1)}, bf16[256,256]{1,0:T(8,128)(2,1)S(1)}, u32[]{:S(2)}, u32[]{:S(2)}) collective-permute-start(bf16[256,256]{1,0:T(8,128)(2,1)S(1)} %get-tuple-element.28), channel_id=1, source_target_pairs={{4,0},{5,1},{6,2},{7,3},{12,8},{13,9},{14,10},{15,11},{20,16},{21,... | collective-permute-start | bytes 393224 | tf_op jit(solution)/shard_map/ppermute | solution.py:17
  71.7 14.9 %collective-permute-start.6 = (bf16[256,256]{1,0:T(8,128)(2,1)S(1)}, bf16[256,256]{1,0:T(8,128)(2,1)S(1)}, u32[]{:S(2)}, u32[]{:S(2)}) collective-permute-start(bf16[256,256]{1,0:T(8,128)(2,1)S(1)} %get-tuple-element.28), channel_id=1, source_target_pairs={{0,4},{1,5},{2,6},{3,7},{8,12},{9,13},{10,14},{11,15},{16,20},{17,... | collective-permute-start | bytes 393224 | tf_op jit(solution)/shard_map/ppermute | solution.py:17
  77.2 11.6 %collective-permute-start.5 = (bf16[256,256]{1,0:T(8,128)(2,1)S(1)}, bf16[256,256]{1,0:T(8,128)(2,1)S(1)}, u32[]{:S(2)}, u32[]{:S(2)}) collective-permute-start(bf16[256,256]{1,0:T(8,128)(2,1)S(1)} %get-tuple-element.28), channel_id=1, source_target_pairs={{1,0},{2,1},{3,2},{4,3},{5,4},{6,5},{7,6},{9,8},{10,9},{11,10},{12... | collective-permute-start | bytes 393224 | tf_op jit(solution)/shard_map/ppermute | solution.py:17
  78.5 12.5 %collective-permute-start.4 = (bf16[256,256]{1,0:T(8,128)(2,1)S(1)}, bf16[256,256]{1,0:T(8,128)(2,1)S(1)}, u32[]{:S(2)}, u32[]{:S(2)}) collective-permute-start(bf16[256,256]{1,0:T(8,128)(2,1)S(1)} %get-tuple-element.28), channel_id=1, source_target_pairs={{0,1},{1,2},{2,3},{3,4},{4,5},{5,6},{6,7},{8,9},{9,10},{10,11},{11... | collective-permute-start | bytes 393224 | tf_op jit(solution)/shard_map/ppermute | solution.py:17
  114.7 24.8 %copy-start.1 = (f32[256,256]{1,0:T(8,128)}, f32[256,256]{1,0:T(8,128)S(1)}, u32[]{:S(2)}) copy-start(f32[256,256]{1,0:T(8,128)S(1)} %get-tuple-element.27) | copy-start | bytes 786436
  114.7 18.1 %collective-permute-start.11 = (bf16[256,256]{1,0:T(8,128)(2,1)S(1)}, bf16[256,256]{1,0:T(8,128)(2,1)S(1)}, u32[]{:S(2)}, u32[]{:S(2)}) collective-permute-start(bf16[256,256]{1,0:T(8,128)(2,1)S(1)} %get-tuple-element.26), channel_id=1, source_target_pairs={{4,0},{5,1},{6,2},{7,3},{12,8},{13,9},{14,10},{15,11},{20,16},{21,... | collective-permute-start | bytes 393224 | tf_op jit(solution)/shard_map/ppermute | solution.py:17
  116.0 19.0 %collective-permute-start.10 = (bf16[256,256]{1,0:T(8,128)(2,1)S(1)}, bf16[256,256]{1,0:T(8,128)(2,1)S(1)}, u32[]{:S(2)}, u32[]{:S(2)}) collective-permute-start(bf16[256,256]{1,0:T(8,128)(2,1)S(1)} %get-tuple-element.26), channel_id=1, source_target_pairs={{0,4},{1,5},{2,6},{3,7},{8,12},{9,13},{10,14},{11,15},{16,20},{17,... | collective-permute-start | bytes 393224 | tf_op jit(solution)/shard_map/ppermute | solution.py:17
  121.5 15.8 %collective-permute-start.9 = (bf16[256,256]{1,0:T(8,128)(2,1)S(1)}, bf16[256,256]{1,0:T(8,128)(2,1)S(1)}, u32[]{:S(2)}, u32[]{:S(2)}) collective-permute-start(bf16[256,256]{1,0:T(8,128)(2,1)S(1)} %get-tuple-element.26), channel_id=1, source_target_pairs={{1,0},{2,1},{3,2},{4,3},{5,4},{6,5},{7,6},{9,8},{10,9},{11,10},{12... | collective-permute-start | bytes 393224 | tf_op jit(solution)/shard_map/ppermute | solution.py:17
  122.8 16.7 %collective-permute-start.8 = (bf16[256,256]{1,0:T(8,128)(2,1)S(1)}, bf16[256,256]{1,0:T(8,128)(2,1)S(1)}, u32[]{:S(2)}, u32[]{:S(2)}) collective-permute-start(bf16[256,256]{1,0:T(8,128)(2,1)S(1)} %get-tuple-element.26), channel_id=1, source_target_pairs={{0,1},{1,2},{2,3},{3,4},{4,5},{5,6},{6,7},{8,9},{9,10},{10,11},{11... | collective-permute-start | bytes 393224 | tf_op jit(solution)/shard_map/ppermute | solution.py:17
  127.0 31.5 %collective-permute-start.12 = (bf16[256,256]{1,0:T(8,128)(2,1)S(1)}, bf16[256,256]{1,0:T(8,128)(2,1)S(1)}, u32[]{:S(2)}, u32[]{:S(2)}) collective-permute-start(bf16[256,256]{1,0:T(8,128)(2,1)S(1)} %get-tuple-element.26), channel_id=1, source_target_pairs={{0,8},{8,16},{16,24},{1,9},{9,17},{17,25},{2,10},{10,18},{18,26},{... | collective-permute-start | bytes 393224 | tf_op jit(solution)/shard_map/ppermute | solution.py:17
where the time goes:
time: 161 us; the launch traced here: 159 us
  blocking collectives  62.6 us (39%)
  matrix products  38.1 us (24%)
  starting transfers between devices  36.6 us (23%)
  between operations  15.9 us (10%)
  other arithmetic  4.15 us (3%)
  local copies, waits for them, and re-layouts  1.93 us (1%)
    psum x3, blocking collectives, body(): lax.psum((jnp.sum(image * image), jnp.sum(image * current), jnp.sum(image...  43.9 us
    ppermute x13, starting transfers between devices, shifted(): return lax.ppermute(block, axis, route)  36.6 us
    dot_general x15, matrix products, contract(): jnp.einsum('wik,wlk->il', inner, right_env[start:stop], preferred_element...  35.9 us
    psum x1, blocking collectives, body(): squared_start = lax.psum(jnp.sum(start_vec * start_vec), 'sec')  18.7 us
  transfers between devices with their start and end apart: 13, of which 0 were waited for; matrix products, arithmetic and copies ran while one was open for 20% of the time, Pallas kernels for 0%

commit v1 on v0

v1 whole, which is shorter than its diff:
```python
import functools

import jax
import jax.numpy as jnp
from jax import lax
from jax.experimental import pallas as pl
from jax.experimental.pallas import tpu as pltpu
from jax.sharding import PartitionSpec as P


W_ZERO = 6
W_HOP = 6
GRID = 4
EPSILON = 1e-06
SCALE = 2.0**-13
ROWS = 16

F32 = jnp.float32
BF16 = jnp.bfloat16


def matchings(count):
    found = {}
    for parity in (0, 1):
        pairs = []
        for s in range(count):
            c = s % GRID
            t = s + 1 if c % 2 == parity else s - 1
            if 0 <= c + (t - s) < GRID:
                pairs.append((s, t))
        if pairs:
            found[f"col{parity}"] = pairs
    for parity in (0, 1):
        pairs = []
        for s in range(count):
            r = s // GRID
            t = s + GRID if r % 2 == parity else s - GRID
            if 0 <= t < count:
                pairs.append((s, t))
        if pairs:
            found[f"row{parity}"] = pairs
    return found


def first_term(name):
    s = lax.axis_index("sec")
    place = lax.rem(s, GRID) if name[:3] == "col" else lax.div(s, GRID)
    ahead = lax.rem(place, 2) == int(name[3])
    base = W_ZERO if name[:3] == "col" else W_ZERO + 2 * W_HOP
    return jnp.where(ahead, base + W_HOP, base)


def contract(left, right, block):
    n, size = left.shape[0], left.shape[1]
    inner = jnp.dot(left.reshape(n * size, size), block, preferred_element_type=F32).astype(BF16)
    across = jnp.concatenate([inner[w * size : (w + 1) * size] for w in range(n)], axis=1)
    beside = jnp.concatenate([right[w] for w in range(n)], axis=1)
    return lax.dot_general(across, beside, (((1,), (1,)), ((), ())), preferred_element_type=F32)


def group(left_ref, right_ref, block, start, n):
    return contract(left_ref[0, 0, pl.ds(start, n)], right_ref[0, 0, pl.ds(start, n)], block)


def masked(value, dims_ref):
    rows = lax.broadcasted_iota(jnp.int32, value.shape, 0)
    cols = lax.broadcasted_iota(jnp.int32, value.shape, 1)
    keep = (rows < dims_ref[0, 0, 0]) & (cols < dims_ref[0, 0, 1])
    return jnp.where(keep, value, 0.0)


def row_sum(a, b):
    return jnp.sum(a * b, axis=0, keepdims=True)


def fold(v):
    out = v[:, :128]
    for k in range(1, v.shape[1] // 128):
        out = out + v[:, k * 128 : (k + 1) * 128]
    return out


def start_kernel(psi_ref, dims_ref, x_ref, low_ref):
    x = masked(psi_ref[0, 0], dims_ref)
    x_ref[...] = x
    low_ref[...] = x.astype(BF16)


def early_kernel(names, left_ref, right_ref, low_ref, *refs):
    blocks, out_ref = refs[:-1], refs[-1]
    total = group(left_ref, right_ref, low_ref[...], 0, W_ZERO)
    for name, ref in zip(names, blocks):
        total = total + group(left_ref, right_ref, ref[...], first_term(name), W_HOP)
    out_ref[...] = total


def late_kernel(names, left_ref, right_ref, dims_ref, total_ref, *refs):
    blocks, u_ref, low_ref = refs[: len(names)], refs[-2], refs[-1]
    total = total_ref[...]
    for name, ref in zip(names, blocks):
        total = total + group(left_ref, right_ref, ref[...], first_term(name), W_HOP)
    u = masked(total * SCALE, dims_ref)
    u_ref[...] = u
    low_ref[...] = u.astype(BF16)


def dots_kernel(u0_ref, u1_ref, u2_ref, u3_ref, out_ref):
    u = [r[...] for r in (u0_ref, u1_ref, u2_ref, u3_ref)]
    out_ref[...] = jnp.zeros_like(out_ref)
    for place, (i, j) in enumerate(PAIRS):
        out_ref[place : place + 1] = fold(row_sum(u[i], u[j]))


PAIRS = [(0, 0), (0, 1), (1, 1), (0, 2), (1, 2), (2, 2), (0, 3), (1, 3), (2, 3)]


def solve(sums, entries):
    table = {}
    for place, (i, j) in enumerate(PAIRS):
        table[i, j] = table[j, i] = jnp.sum(sums[place : place + 1], axis=(0, 1), keepdims=True)
    zero = jnp.zeros((1, 1), F32)

    def dot(c, d):
        out = zero
        for i, a in enumerate(c):
            for j, b in enumerate(d):
                if a is not None and b is not None:
                    out = out + a * b * table[i, j]
        return out

    def apply(c):
        return [None] + [None if a is None else a * (1.0 / SCALE) for a in c]

    inv = 1.0 / entries
    v0 = [1.0 / jnp.sqrt(table[0, 0] * inv + EPSILON)]
    w = apply(v0)
    alpha0 = dot(w, v0) * inv
    r = [-alpha0 * v0[0], w[1]]
    beta0 = jnp.sqrt(dot(r, r) * inv + EPSILON)
    second = [c / beta0 for c in r]
    w = apply(second)
    alpha1 = dot(w, second) * inv
    r = [-alpha1 * second[0] - beta0 * v0[0], w[1] - alpha1 * second[1], w[2]]
    beta1 = jnp.sqrt(dot(r, r) * inv + EPSILON)
    third = [c / beta1 for c in r]
    image = apply(third)
    alpha2 = dot(image, third) * inv
    return second, third, image, [alpha0, alpha1, alpha2, beta0, beta1]


def combine(coefs, refs):
    out = None
    for c, r in zip(coefs, refs):
        if c is not None:
            out = c * r[...] if out is None else out + c * r[...]
    return out


def third_kernel(entries, sums_ref, u0_ref, u1_ref, u2_ref, third_ref, own_ref):
    _, coefs, _, _ = solve(sums_ref[...], entries)
    third = combine(coefs, (u0_ref, u1_ref, u2_ref))
    third_ref[0, 0] = third
    own_ref[...] = third.astype(BF16)


def rest_kernel(
    entries, sums_ref, u0_ref, u1_ref, u2_ref, u3_ref, left_ref, own_ref,
    second_ref, image_ref, coef_ref, env_ref,
):
    second, _, image, values = solve(sums_ref[...], entries)
    us = (u0_ref, u1_ref, u2_ref, u3_ref)
    second_ref[0, 0] = combine(second, us)
    image_ref[0, 0] = combine(image, us)
    for place, value in enumerate(values):
        coef_ref[:, place : place + 1] = value
    env_ref[...] = jnp.dot(
        left_ref[0, 0, 0], own_ref[...], preferred_element_type=F32
    ).astype(BF16)


def boundary_kernel(own_ref, before_ref, env_ref, out_ref):
    dims = (((0,), (0,)), ((), ()))
    total = lax.dot_general(own_ref[...], env_ref[...], dims, preferred_element_type=F32)
    total = total + lax.dot_general(
        before_ref[...], env_ref[...], dims, preferred_element_type=F32
    )
    out_ref[0, 0] = total * (1.0 / total.shape[0] ** 0.5)


def kernel_call(body, out_shape, spaces, flops):
    def spec(space):
        return pl.BlockSpec(memory_space=space)

    return pl.pallas_call(
        body,
        out_shape=out_shape,
        in_specs=[spec(pltpu.SMEM if s == "s" else pltpu.VMEM) for s in spaces],
        out_specs=jax.tree.map(lambda _: spec(pltpu.VMEM), out_shape),
        compiler_params=pltpu.CompilerParams(vmem_limit_bytes=24 << 20),
        cost_estimate=pl.CostEstimate(flops=flops, bytes_accessed=0, transcendentals=0),
    )


def body(psi, sector_dims, env_left, env_right):
    size = psi.shape[-1]
    count = lax.axis_size("sec")
    entries = float(count * size * size)
    block32 = jax.ShapeDtypeStruct((size, size), F32)
    block16 = jax.ShapeDtypeStruct((size, size), BF16)
    swaps = matchings(count)
    early = [n for n in swaps if n == "col0"]
    late = [n for n in swaps if n[:3] == "row"] + [n for n in swaps if n == "col1"]
    sent = [n for n in swaps if n[:3] == "row"] + [n for n in swaps if n[:3] == "col"]
    product = 2 * 2 * size**3

    x, low = kernel_call(start_kernel, (block32, block16), "vs", 0)(psi, sector_dims)
    vectors = [x]
    for _ in range(3):
        found = {}
        for n in sent:
            found[n] = lax.ppermute(low, "sec", swaps[n])
        total = kernel_call(
            functools.partial(early_kernel, early),
            block32,
            "vvv" + "v" * len(early),
            product * (W_ZERO + W_HOP * len(early)),
        )(env_left, env_right, low, *[found[n] for n in early])
        u, low = kernel_call(
            functools.partial(late_kernel, late),
            (block32, block16),
            "vvsv" + "v" * len(late),
            product * W_HOP * len(late),
        )(env_left, env_right, sector_dims, total, *[found[n] for n in late])
        vectors.append(u)
    sums = kernel_call(dots_kernel, jax.ShapeDtypeStruct((ROWS, 128), F32), "vvvv", 0)(*vectors)
    hop = 1
    while hop < count:
        sums = sums + lax.ppermute(sums, "sec", [(i, i ^ hop) for i in range(count)])
        hop *= 2
    full = jax.ShapeDtypeStruct((1, 1, size, size), F32)
    third, own = kernel_call(
        functools.partial(third_kernel, entries), (full, block16), "vvvv", 0
    )(sums, *vectors[:3])
    segs = lax.axis_size("seg")
    before = lax.ppermute(own, "seg", [(g, g + 1) for g in range(segs - 1)])
    second, image, coefs, env = kernel_call(
        functools.partial(rest_kernel, entries),
        (full, full, jax.ShapeDtypeStruct((1, 5), F32), block16),
        "vvvvvvv",
        2 * size**3,
    )(sums, *vectors, env_left, own)
    boundary = kernel_call(boundary_kernel, full, "vvv", 4 * size**3)(
        own, before, env
    )
    return second, third, image, coefs, boundary


def solution(mesh):
    count = mesh.shape["sec"]
    assert count & (count - 1) == 0
    in_specs = (
        P("seg", "sec", None, None),
        P("seg", "sec", None),
        P("seg", "sec", None, None, None),
        P("seg", "sec", None, None, None),
    )
    out_specs = (
        P("seg", "sec", None, None),
        P("seg", "sec", None, None),
        P("seg", "sec", None, None),
        P("seg", None),
        P("seg", "sec", None, None),
    )
    return jax.shard_map(body, mesh=mesh, in_specs=in_specs, out_specs=out_specs, check_vma=False)
```

time: 161 us -> 61.5 us (0.38)
  blocking collectives: 62.6 us -> 0 us
  matrix products: 38.1 us -> 0 us
  waiting for transfers between devices: 0.03 us -> 24.4 us
  starting transfers between devices: 36.6 us -> 14.2 us
  between operations: 15.9 us -> 0.78 us
  Pallas kernels: 0 us -> 13.9 us
  local copies, waits for them, and re-layouts: 1.93 us -> 7.64 us
  other arithmetic: 4.15 us -> 0.01 us
    psum x4 -> x0, blocking collectives: 62.6 us -> none  [the longest x3 43.9 us: body(): lax.psum((jnp.sum(image * image), jnp.sum(image * current), jnp.sum(image...]
    dot_general x18 -> x0, matrix products: 38.1 us -> none  [the longest x15 35.9 us: contract(): jnp.einsum('wik,wlk->il', inner, right_env[start:stop], preferred_element...]
    ppermute x13, waiting for transfers between devices: 0.03 us -> 24.4 us  [the longest x9 14.5 us: body(): found[n] = lax.ppermute(low, 'sec', swaps[n])]
    ppermute x13, starting transfers between devices: 36.6 us -> 14.2 us  [the longest x9 9.82 us: body(): found[n] = lax.ppermute(low, 'sec', swaps[n])]
    pallas_call x0 -> x11, Pallas kernels: none -> 13.9 us  [the longest x3 5.54 us: body(): kernel_call(functools.partial(late_kernel, late), (block32, block16), 'vv...]
    unnamed x4 -> x14, local copies, waits for them, and re-layouts: 0.01 us -> 7.64 us
    reduce_sum x1 -> x0, other arithmetic: 1.7 us -> none  [body(): squared_start = lax.psum(jnp.sum(start_vec * start_vec), 'sec')]
  transfers between devices with their start and end apart: 13 -> 13, of which waited for: 0 -> 7; matrix products, arithmetic and copies ran while one was open for 20% -> 0% of each run, Pallas kernels for 0% -> 9%
where the time goes in v1:
time: 61.5 us; the launch traced here: 60.9 us
  waiting for transfers between devices  24.4 us (40%)
  starting transfers between devices  14.2 us (23%)
  Pallas kernels  13.9 us (23%)
  local copies, waits for them, and re-layouts  7.64 us (12%)
  between operations  0.78 us (1%)
    ppermute x9, waiting for transfers between devices, body(): found[n] = lax.ppermute(low, 'sec', swaps[n])  14.5 us
    ppermute x9, starting transfers between devices, body(): found[n] = lax.ppermute(low, 'sec', swaps[n])  9.82 us
    ppermute x3, waiting for transfers between devices, body(): lax.ppermute(sums, 'sec', [(i, i ^ hop) for i in range(count)])  8.53 us
    unnamed x14, local copies, waits for them, and re-layouts  7.64 us
    pallas_call x3, Pallas kernels, body(): kernel_call(functools.partial(late_kernel, late), (block32, block16), 'vv...  5.54 us
    pallas_call x3, Pallas kernels, body(): kernel_call(functools.partial(early_kernel, early), block32, 'vvv' + 'v'...  4.41 us
    ppermute x1, starting transfers between devices, body(): before = lax.ppermute(own, 'seg', [(g, g + 1) for g in range(segs - 1)])  3.39 us
    ppermute x1, waiting for transfers between devices, body(): before = lax.ppermute(own, 'seg', [(g, g + 1) for g in range(segs - 1)])  1.37 us
  transfers between devices with their start and end apart: 13, of which 7 were waited for; matrix products, arithmetic and copies ran while one was open for 0% of the time, Pallas kernels for 9%

profile of v1, /device:TPU:0, one launch (start us, length us, event | category | flops | bytes accessed | tf_op | source)
XLA Modules:
  0.0 60.9 jit_solution(17908507988492933571)
XLA Ops:
  0.6 0.0 copy-start.4
  0.6 0.9 %copy-done.4 = f32[1,1,256,256]{3,2,1,0:T(8,128)S(1)} copy-done((f32[1,1,256,256]{3,2,1,0:T(8,128)S(1)}, f32[1,1,256,256]{3,2,1,0:T(8,128)}, u32[]{:S(2)}) %copy-start.4) | copy-done | bytes 262168
  1.6 0.0 copy-start.5
  1.6 0.7 %copy-done.5 = s32[1,1,2]{2,1,0:T(1,128)S(1)} copy-done((s32[1,1,2]{2,1,0:T(1,128)S(1)}, s32[1,1,2]{2,1,0:T(1,128)}, u32[]{:S(2)}) %copy-start.5) | copy-done | bytes 32
  2.2 0.6 shard_map.83
  2.8 0.0 copy-start.6
  2.8 0.6 collective-permute-start
  3.4 0.7 %collective-permute-start.2 = (bf16[256,256]{1,0:T(8,128)(2,1)S(1)}, bf16[256,256]{1,0:T(8,128)(2,1)S(1)}, u32[]{:S(2)}, u32[]{:S(2)}) collective-permute-start(bf16[256,256]{1,0:T(8,128)(2,1)S(1)} %get-tuple-element.19.low_ref), channel_id=1, source_target_pairs={{1,2},{2,1},{5,6},{6,5},{9,10},{10,9},{13,14},{14,13},{17,18},{18,... | collective-permute-start | bytes 393224 | tf_op jit(solution)/shard_map/ppermute | solution.py:221
  4.1 3.7 %collective-permute-start.1 = (bf16[256,256]{1,0:T(8,128)(2,1)S(1)}, bf16[256,256]{1,0:T(8,128)(2,1)S(1)}, u32[]{:S(2)}, u32[]{:S(2)}) collective-permute-start(bf16[256,256]{1,0:T(8,128)(2,1)S(1)} %get-tuple-element.19.low_ref), channel_id=1, source_target_pairs={{0,4},{1,5},{2,6},{3,7},{4,0},{5,1},{6,2},{7,3},{8,12},{9,13},{10,... | collective-permute-start | bytes 393224 | tf_op jit(solution)/shard_map/ppermute | solution.py:221
  7.7 0.0 collective-permute-done.refs_0_
  7.7 0.0 copy-start
  7.7 2.1 %copy-done = bf16[1,1,30,256,256]{4,3,2,1,0:T(8,128)(2,1)S(1)} copy-done((bf16[1,1,30,256,256]{4,3,2,1,0:T(8,128)(2,1)S(1)}, bf16[1,1,30,256,256]{4,3,2,1,0:T(8,128)(2,1)}, u32[]{:S(2)}) %copy-start) | copy-done | bytes 3932184
  9.8 0.0 copy-start.2
  9.8 2.1 %copy-done.2 = bf16[1,1,30,256,256]{4,3,2,1,0:T(8,128)(2,1)S(1)} copy-done((bf16[1,1,30,256,256]{4,3,2,1,0:T(8,128)(2,1)S(1)}, bf16[1,1,30,256,256]{4,3,2,1,0:T(8,128)(2,1)}, u32[]{:S(2)}) %copy-start.2) | copy-done | bytes 3932184
  12.0 0.0 copy-start.1
  12.0 0.0 copy-start.3
  12.0 1.5 %shard_map.84.total_ref = f32[256,256]{1,0:T(8,128)S(1)} custom-call(bf16[1,1,30,256,256]{4,3,2,1,0:T(8,128)(2,1)S(1)} %copy-done, bf16[1,1,30,256,256]{4,3,2,1,0:T(8,128)(2,1)S(1)} %copy-done.2, bf16[256,256]{1,0:T(8,128)(2,1)S(1)} %get-tuple-element.19.low_ref, bf16[256,256]{1,0:T(8,128)(2,1)S(1)} %collective-permute-done.refs_0_), custom_call_target="tpu_custom_call" | custom-call | flops 805306368 | tf_op jit(solution)/shard_map/pallas_call | solution.py:222
  13.4 0.0 collective-permute-done.2.refs_1_
  13.4 0.0 collective-permute-done.1.refs_0_
  13.5 0.0 copy-done.6
  13.5 0.6 copy-done.1
  14.1 1.2 %copy-done.3 = bf16[1,1,30,256,256]{4,3,2,1,0:T(8,128)(2,1)S(1)} copy-done((bf16[1,1,30,256,256]{4,3,2,1,0:T(8,128)(2,1)S(1)}, bf16[1,1,30,256,256]{4,3,2,1,0:T(8,128)(2,1)}, u32[]{:S(2)}) %copy-start.3) | copy-done | bytes 3932184
  15.3 1.6 %shard_map.85 = (f32[256,256]{1,0:T(8,128)S(1)}, bf16[256,256]{1,0:T(8,128)(2,1)S(1)}) custom-call(bf16[1,1,30,256,256]{4,3,2,1,0:T(8,128)(2,1)S(1)} %copy-done.1, bf16[1,1,30,256,256]{4,3,2,1,0:T(8,128)(2,1)S(1)} %copy-done.3, s32[1,1,2]{2,1,0:T(1,128)S(1)} %copy-done.6, f32[256,256]{1,0:T(8,128)S(1)} %shard_map.84.total_ref, ...), custom_call_target="tpu_custom_call" | custom-call | flops 805306368 | tf_op jit(solution)/shard_map/pallas_call | solution.py:228
  16.9 2.7 %collective-permute-start.3 = (bf16[256,256]{1,0:T(8,128)(2,1)S(1)}, bf16[256,256]{1,0:T(8,128)(2,1)S(1)}, u32[]{:S(2)}, u32[]{:S(2)}) collective-permute-start(bf16[256,256]{1,0:T(8,128)(2,1)S(1)} %get-tuple-element.21.low_ref), channel_id=1, source_target_pairs={{0,1},{1,0},{2,3},{3,2},{4,5},{5,4},{6,7},{7,6},{8,9},{9,8},{10,11... | collective-permute-start | bytes 393224 | tf_op jit(solution)/shard_map/ppermute | solution.py:221
  19.6 0.7 %collective-permute-start.5 = (bf16[256,256]{1,0:T(8,128)(2,1)S(1)}, bf16[256,256]{1,0:T(8,128)(2,1)S(1)}, u32[]{:S(2)}, u32[]{:S(2)}) collective-permute-start(bf16[256,256]{1,0:T(8,128)(2,1)S(1)} %get-tuple-element.21.low_ref), channel_id=1, source_target_pairs={{1,2},{2,1},{5,6},{6,5},{9,10},{10,9},{13,14},{14,13},{17,18},{18,... | collective-permute-start | bytes 393224 | tf_op jit(solution)/shard_map/ppermute | solution.py:221
  20.3 0.4 collective-permute-start.4
  20.7 0.0 collective-permute-done.3.refs_0_
  20.7 1.5 %shard_map.86.total_ref = f32[256,256]{1,0:T(8,128)S(1)} custom-call(bf16[1,1,30,256,256]{4,3,2,1,0:T(8,128)(2,1)S(1)} %copy-done.1, bf16[1,1,30,256,256]{4,3,2,1,0:T(8,128)(2,1)S(1)} %copy-done.3, bf16[256,256]{1,0:T(8,128)(2,1)S(1)} %get-tuple-element.21.low_ref, bf16[256,256]{1,0:T(8,128)(2,1)S(1)} %collective-permute-done.3.refs_0_), custom_call_target="tpu_custom_call" | custom-call | flops 805306368 | tf_op jit(solution)/shard_map/pallas_call | solution.py:222
  22.2 0.0 collective-permute-done.5.refs_1_
  22.2 7.5 %collective-permute-done.4.refs_0_ = bf16[256,256]{1,0:T(8,128)(2,1)S(1)} collective-permute-done((bf16[256,256]{1,0:T(8,128)(2,1)S(1)}, bf16[256,256]{1,0:T(8,128)(2,1)S(1)}, u32[]{:S(2)}, u32[]{:S(2)}) %collective-permute-start.4) | collective-permute-done | bytes 131104 | tf_op jit(solution)/shard_map/ppermute | solution.py:221
  29.7 1.6 %shard_map.87 = (f32[256,256]{1,0:T(8,128)S(1)}, bf16[256,256]{1,0:T(8,128)(2,1)S(1)}) custom-call(bf16[1,1,30,256,256]{4,3,2,1,0:T(8,128)(2,1)S(1)} %copy-done.1, bf16[1,1,30,256,256]{4,3,2,1,0:T(8,128)(2,1)S(1)} %copy-done.3, s32[1,1,2]{2,1,0:T(1,128)S(1)} %copy-done.6, f32[256,256]{1,0:T(8,128)S(1)} %shard_map.86.total_ref, ...), custom_call_target="tpu_custom_call" | custom-call | flops 805306368 | tf_op jit(solution)/shard_map/pallas_call | solution.py:228
  31.3 0.4 collective-permute-start.6
  31.8 0.7 %collective-permute-start.8 = (bf16[256,256]{1,0:T(8,128)(2,1)S(1)}, bf16[256,256]{1,0:T(8,128)(2,1)S(1)}, u32[]{:S(2)}, u32[]{:S(2)}) collective-permute-start(bf16[256,256]{1,0:T(8,128)(2,1)S(1)} %get-tuple-element.23.low_ref), channel_id=1, source_target_pairs={{1,2},{2,1},{5,6},{6,5},{9,10},{10,9},{13,14},{14,13},{17,18},{18,... | collective-permute-start | bytes 393224 | tf_op jit(solution)/shard_map/ppermute | solution.py:221
  32.5 0.1 collective-permute-start.7
  32.5 0.2 collective-permute-done.6.refs_0_
  32.8 1.5 %shard_map.88.total_ref = f32[256,256]{1,0:T(8,128)S(1)} custom-call(bf16[1,1,30,256,256]{4,3,2,1,0:T(8,128)(2,1)S(1)} %copy-done.1, bf16[1,1,30,256,256]{4,3,2,1,0:T(8,128)(2,1)S(1)} %copy-done.3, bf16[256,256]{1,0:T(8,128)(2,1)S(1)} %get-tuple-element.23.low_ref, bf16[256,256]{1,0:T(8,128)(2,1)S(1)} %collective-permute-done.6.refs_0_), custom_call_target="tpu_custom_call" | custom-call | flops 805306368 | tf_op jit(solution)/shard_map/pallas_call | solution.py:222
  34.3 0.0 collective-permute-done.8.refs_1_
  34.3 6.7 %collective-permute-done.7.refs_0_ = bf16[256,256]{1,0:T(8,128)(2,1)S(1)} collective-permute-done((bf16[256,256]{1,0:T(8,128)(2,1)S(1)}, bf16[256,256]{1,0:T(8,128)(2,1)S(1)}, u32[]{:S(2)}, u32[]{:S(2)}) %collective-permute-start.7) | collective-permute-done | bytes 131104 | tf_op jit(solution)/shard_map/ppermute | solution.py:221
  40.9 2.3 %shard_map.89 = (f32[256,256]{1,0:T(8,128)S(1)}, bf16[256,256]{1,0:T(8,128)(2,1)}) custom-call(bf16[1,1,30,256,256]{4,3,2,1,0:T(8,128)(2,1)S(1)} %copy-done.1, bf16[1,1,30,256,256]{4,3,2,1,0:T(8,128)(2,1)S(1)} %copy-done.3, s32[1,1,2]{2,1,0:T(1,128)S(1)} %copy-done.6, f32[256,256]{1,0:T(8,128)S(1)} %shard_map.88.total_ref, ...), custom_call_target="tpu_custom_call" | custom-call | flops 805306368 | tf_op jit(solution)/shard_map/pallas_call | solution.py:228
  43.2 0.2 shard_map.90
  43.5 0.2 collective-permute-start.9
  43.7 1.0 %collective-permute-done.9 = f32[16,128]{1,0:T(8,128)S(1)} collective-permute-done((f32[16,128]{1,0:T(8,128)S(1)}, f32[16,128]{1,0:T(8,128)S(1)}, u32[]{:S(2)}, u32[]{:S(2)}) %collective-permute-start.9) | collective-permute-done | bytes 8224 | tf_op jit(solution)/shard_map/ppermute | solution.py:238
  44.7 0.6 collective-permute-start.10
  45.3 3.1 %collective-permute-done.10 = f32[16,128]{1,0:T(8,128)S(1)} collective-permute-done((f32[16,128]{1,0:T(8,128)S(1)}, f32[16,128]{1,0:T(8,128)S(1)}, u32[]{:S(2)}, u32[]{:S(2)}) %collective-permute-start.10) | collective-permute-done | bytes 8224 | tf_op jit(solution)/shard_map/ppermute | solution.py:238
  48.4 0.2 collective-permute-start.11
  48.5 4.4 %collective-permute-done.11 = f32[16,128]{1,0:T(8,128)S(1)} collective-permute-done((f32[16,128]{1,0:T(8,128)S(1)}, f32[16,128]{1,0:T(8,128)S(1)}, u32[]{:S(2)}, u32[]{:S(2)}) %collective-permute-start.11) | collective-permute-done | bytes 8224 | tf_op jit(solution)/shard_map/ppermute | solution.py:238
  53.0 1.0 %shard_map.91 = (f32[1,1,256,256]{3,2,1,0:T(8,128)}, bf16[256,256]{1,0:T(8,128)(2,1)S(1)}) custom-call(f32[16,128]{1,0:T(8,128)S(1)} %add.11.sums_ref, f32[256,256]{1,0:T(8,128)S(1)} %get-tuple-element.18.u0_ref, f32[256,256]{1,0:T(8,128)S(1)} %get-tuple-element.20.u1_ref, f32[256,256]{1,0:T(8,128)S(1)} %get-tuple-element.22.u2_ref), custom_call_target="tpu_custom_call" | custom-call | tf_op jit(solution)/shard_map/pallas_call | solution.py:241
  54.0 3.4 %collective-permute-start.12 = (bf16[256,256]{1,0:T(8,128)(2,1)S(1)}, bf16[256,256]{1,0:T(8,128)(2,1)S(1)}, u32[]{:S(2)}, u32[]{:S(2)}) collective-permute-start(bf16[256,256]{1,0:T(8,128)(2,1)S(1)} %get-tuple-element.25.own_ref), channel_id=1, source_target_pairs={{0,8},{8,16},{16,24},{1,9},{9,17},{17,25},{2,10},{10,18},{18,26},{... | collective-permute-start | bytes 393224 | tf_op jit(solution)/shard_map/ppermute | solution.py:245
  57.4 1.1 %shard_map.92 = (f32[1,1,256,256]{3,2,1,0:T(8,128)}, f32[1,1,256,256]{3,2,1,0:T(8,128)}, f32[1,5]{1,0:T(1,128)}, bf16[256,256]{1,0:T(8,128)(2,1)S(1)}) custom-call(f32[16,128]{1,0:T(8,128)S(1)} %add.11.sums_ref, f32[256,256]{1,0:T(8,128)S(1)} %get-tuple-element.18.u0_ref, f32[256,256]{1,0:T(8,128)S(1)} %get-tuple-element.20.u1_ref, ...), custom_call_target="tpu_custom_call" | custom-call | flops 33554432 | tf_op jit(solution)/shard_map/pallas_call | solution.py:246
  58.5 1.4 %collective-permute-done.12.before_ref = bf16[256,256]{1,0:T(8,128)(2,1)S(1)} collective-permute-done((bf16[256,256]{1,0:T(8,128)(2,1)S(1)}, bf16[256,256]{1,0:T(8,128)(2,1)S(1)}, u32[]{:S(2)}, u32[]{:S(2)}) %collective-permute-start.12) | collective-permute-done | bytes 131104 | tf_op jit(solution)/shard_map/ppermute | solution.py:245
  59.9 1.0 %shard_map.93 = f32[1,1,256,256]{3,2,1,0:T(8,128)} custom-call(bf16[256,256]{1,0:T(8,128)(2,1)S(1)} %get-tuple-element.25.own_ref, bf16[256,256]{1,0:T(8,128)(2,1)S(1)} %collective-permute-done.12.before_ref, bf16[256,256]{1,0:T(8,128)(2,1)S(1)} %get-tuple-element.30.env_ref), custom_call_target="tpu_custom_call" | custom-call | flops 67108864 | tf_op jit(solution)/shard_map/pallas_call | solution.py:252
  (3 shorter events, 0.0 us)
Async XLA Ops:
  0.6 1.0 %copy-start.4 = (f32[1,1,256,256]{3,2,1,0:T(8,128)S(1)}, f32[1,1,256,256]{3,2,1,0:T(8,128)}, u32[]{:S(2)}) copy-start(f32[1,1,256,256]{3,2,1,0:T(8,128)} %psi_ref.1) | copy-start | bytes 786436
  1.6 0.7 %copy-start.5 = (s32[1,1,2]{2,1,0:T(1,128)S(1)}, s32[1,1,2]{2,1,0:T(1,128)}, u32[]{:S(2)}) copy-start(s32[1,1,2]{2,1,0:T(1,128)} %dims_ref.7) | copy-start | bytes 28
  2.8 10.6 %copy-start.6 = (s32[1,1,2]{2,1,0:T(1,128)S(1)}, s32[1,1,2]{2,1,0:T(1,128)}, u32[]{:S(2)}) copy-start(s32[1,1,2]{2,1,0:T(1,128)} %dims_ref.7) | copy-start | bytes 28
  2.8 4.9 %collective-permute-start = (bf16[256,256]{1,0:T(8,128)(2,1)S(1)}, bf16[256,256]{1,0:T(8,128)(2,1)S(1)}, u32[]{:S(2)}, u32[]{:S(2)}) collective-permute-start(bf16[256,256]{1,0:T(8,128)(2,1)S(1)} %get-tuple-element.19.low_ref), channel_id=1, source_target_pairs={{0,1},{1,0},{2,3},{3,2},{4,5},{5,4},{6,7},{7,6},{8,9},{9,8},{10,11... | collective-permute-start | bytes 393224 | tf_op jit(solution)/shard_map/ppermute | solution.py:221
  3.4 10.0 %collective-permute-start.2 = (bf16[256,256]{1,0:T(8,128)(2,1)S(1)}, bf16[256,256]{1,0:T(8,128)(2,1)S(1)}, u32[]{:S(2)}, u32[]{:S(2)}) collective-permute-start(bf16[256,256]{1,0:T(8,128)(2,1)S(1)} %get-tuple-element.19.low_ref), channel_id=1, source_target_pairs={{1,2},{2,1},{5,6},{6,5},{9,10},{10,9},{13,14},{14,13},{17,18},{18,... | collective-permute-start | bytes 393224 | tf_op jit(solution)/shard_map/ppermute | solution.py:221
  4.1 9.4 %collective-permute-start.1 = (bf16[256,256]{1,0:T(8,128)(2,1)S(1)}, bf16[256,256]{1,0:T(8,128)(2,1)S(1)}, u32[]{:S(2)}, u32[]{:S(2)}) collective-permute-start(bf16[256,256]{1,0:T(8,128)(2,1)S(1)} %get-tuple-element.19.low_ref), channel_id=1, source_target_pairs={{0,4},{1,5},{2,6},{3,7},{4,0},{5,1},{6,2},{7,3},{8,12},{9,13},{10,... | collective-permute-start | bytes 393224 | tf_op jit(solution)/shard_map/ppermute | solution.py:221
  7.7 2.1 %copy-start = (bf16[1,1,30,256,256]{4,3,2,1,0:T(8,128)(2,1)S(1)}, bf16[1,1,30,256,256]{4,3,2,1,0:T(8,128)(2,1)}, u32[]{:S(2)}) copy-start(bf16[1,1,30,256,256]{4,3,2,1,0:T(8,128)(2,1)} %left_ref.13) | copy-start | bytes 11796484
  9.8 2.1 %copy-start.2 = (bf16[1,1,30,256,256]{4,3,2,1,0:T(8,128)(2,1)S(1)}, bf16[1,1,30,256,256]{4,3,2,1,0:T(8,128)(2,1)}, u32[]{:S(2)}) copy-start(bf16[1,1,30,256,256]{4,3,2,1,0:T(8,128)(2,1)} %right_ref.11) | copy-start | bytes 11796484
  12.0 2.1 %copy-start.1 = (bf16[1,1,30,256,256]{4,3,2,1,0:T(8,128)(2,1)S(1)}, bf16[1,1,30,256,256]{4,3,2,1,0:T(8,128)(2,1)}, u32[]{:S(2)}) copy-start(bf16[1,1,30,256,256]{4,3,2,1,0:T(8,128)(2,1)} %left_ref.13) | copy-start | bytes 11796484
  12.0 3.3 %copy-start.3 = (bf16[1,1,30,256,256]{4,3,2,1,0:T(8,128)(2,1)S(1)}, bf16[1,1,30,256,256]{4,3,2,1,0:T(8,128)(2,1)}, u32[]{:S(2)}) copy-start(bf16[1,1,30,256,256]{4,3,2,1,0:T(8,128)(2,1)} %right_ref.11) | copy-start | bytes 11796484
  16.9 3.8 %collective-permute-start.3 = (bf16[256,256]{1,0:T(8,128)(2,1)S(1)}, bf16[256,256]{1,0:T(8,128)(2,1)S(1)}, u32[]{:S(2)}, u32[]{:S(2)}) collective-permute-start(bf16[256,256]{1,0:T(8,128)(2,1)S(1)} %get-tuple-element.21.low_ref), channel_id=1, source_target_pairs={{0,1},{1,0},{2,3},{3,2},{4,5},{5,4},{6,7},{7,6},{8,9},{9,8},{10,11... | collective-permute-start | bytes 393224 | tf_op jit(solution)/shard_map/ppermute | solution.py:221
  19.6 2.5 %collective-permute-start.5 = (bf16[256,256]{1,0:T(8,128)(2,1)S(1)}, bf16[256,256]{1,0:T(8,128)(2,1)S(1)}, u32[]{:S(2)}, u32[]{:S(2)}) collective-permute-start(bf16[256,256]{1,0:T(8,128)(2,1)S(1)} %get-tuple-element.21.low_ref), channel_id=1, source_target_pairs={{1,2},{2,1},{5,6},{6,5},{9,10},{10,9},{13,14},{14,13},{17,18},{18,... | collective-permute-start | bytes 393224 | tf_op jit(solution)/shard_map/ppermute | solution.py:221
  20.3 9.4 %collective-permute-start.4 = (bf16[256,256]{1,0:T(8,128)(2,1)S(1)}, bf16[256,256]{1,0:T(8,128)(2,1)S(1)}, u32[]{:S(2)}, u32[]{:S(2)}) collective-permute-start(bf16[256,256]{1,0:T(8,128)(2,1)S(1)} %get-tuple-element.21.low_ref), channel_id=1, source_target_pairs={{0,4},{1,5},{2,6},{3,7},{4,0},{5,1},{6,2},{7,3},{8,12},{9,13},{10,... | collective-permute-start | bytes 393224 | tf_op jit(solution)/shard_map/ppermute | solution.py:221
  31.3 1.4 %collective-permute-start.6 = (bf16[256,256]{1,0:T(8,128)(2,1)S(1)}, bf16[256,256]{1,0:T(8,128)(2,1)S(1)}, u32[]{:S(2)}, u32[]{:S(2)}) collective-permute-start(bf16[256,256]{1,0:T(8,128)(2,1)S(1)} %get-tuple-element.23.low_ref), channel_id=1, source_target_pairs={{0,1},{1,0},{2,3},{3,2},{4,5},{5,4},{6,7},{7,6},{8,9},{9,8},{10,11... | collective-permute-start | bytes 393224 | tf_op jit(solution)/shard_map/ppermute | solution.py:221
  31.8 2.5 %collective-permute-start.8 = (bf16[256,256]{1,0:T(8,128)(2,1)S(1)}, bf16[256,256]{1,0:T(8,128)(2,1)S(1)}, u32[]{:S(2)}, u32[]{:S(2)}) collective-permute-start(bf16[256,256]{1,0:T(8,128)(2,1)S(1)} %get-tuple-element.23.low_ref), channel_id=1, source_target_pairs={{1,2},{2,1},{5,6},{6,5},{9,10},{10,9},{13,14},{14,13},{17,18},{18,... | collective-permute-start | bytes 393224 | tf_op jit(solution)/shard_map/ppermute | solution.py:221
  32.5 8.5 %collective-permute-start.7 = (bf16[256,256]{1,0:T(8,128)(2,1)S(1)}, bf16[256,256]{1,0:T(8,128)(2,1)S(1)}, u32[]{:S(2)}, u32[]{:S(2)}) collective-permute-start(bf16[256,256]{1,0:T(8,128)(2,1)S(1)} %get-tuple-element.23.low_ref), channel_id=1, source_target_pairs={{0,4},{1,5},{2,6},{3,7},{4,0},{5,1},{6,2},{7,3},{8,12},{9,13},{10,... | collective-permute-start | bytes 393224 | tf_op jit(solution)/shard_map/ppermute | solution.py:221
  43.5 1.2 %collective-permute-start.9 = (f32[16,128]{1,0:T(8,128)S(1)}, f32[16,128]{1,0:T(8,128)S(1)}, u32[]{:S(2)}, u32[]{:S(2)}) collective-permute-start(f32[16,128]{1,0:T(8,128)S(1)} %shard_map.90), channel_id=1, source_target_pairs={{0,1},{1,0},{2,3},{3,2},{4,5},{5,4},{6,7},{7,6},{8,9},{9,8},{10,11... | collective-permute-start | bytes 24584 | tf_op jit(solution)/shard_map/ppermute | solution.py:238
  44.7 3.7 %collective-permute-start.10 = (f32[16,128]{1,0:T(8,128)S(1)}, f32[16,128]{1,0:T(8,128)S(1)}, u32[]{:S(2)}, u32[]{:S(2)}) collective-permute-start(f32[16,128]{1,0:T(8,128)S(1)} %add.9), channel_id=1, source_target_pairs={{0,2},{1,3},{2,0},{3,1},{4,6},{5,7},{6,4},{7,5},{8,10},{9,11},{10,... | collective-permute-start | bytes 24584 | tf_op jit(solution)/shard_map/ppermute | solution.py:238
  48.4 4.6 %collective-permute-start.11 = (f32[16,128]{1,0:T(8,128)S(1)}, f32[16,128]{1,0:T(8,128)S(1)}, u32[]{:S(2)}, u32[]{:S(2)}) collective-permute-start(f32[16,128]{1,0:T(8,128)S(1)} %add.10), channel_id=1, source_target_pairs={{0,4},{1,5},{2,6},{3,7},{4,0},{5,1},{6,2},{7,3},{8,12},{9,13},{10,... | collective-permute-start | bytes 24584 | tf_op jit(solution)/shard_map/ppermute | solution.py:238
  54.0 5.9 %collective-permute-start.12 = (bf16[256,256]{1,0:T(8,128)(2,1)S(1)}, bf16[256,256]{1,0:T(8,128)(2,1)S(1)}, u32[]{:S(2)}, u32[]{:S(2)}) collective-permute-start(bf16[256,256]{1,0:T(8,128)(2,1)S(1)} %get-tuple-element.25.own_ref), channel_id=1, source_target_pairs={{0,8},{8,16},{16,24},{1,9},{9,17},{17,25},{2,10},{10,18},{18,26},{... | collective-permute-start | bytes 393224 | tf_op jit(solution)/shard_map/ppermute | solution.py:245

commit v2 on v0

v2 whole, which is shorter than its diff:
```python
import functools

import jax
import jax.numpy as jnp
from jax import lax
from jax.experimental import pallas as pl
from jax.experimental.pallas import tpu as pltpu
from jax.sharding import PartitionSpec as P


W_ZERO = 6
W_HOP = 6
GRID = 4
EPSILON = 1e-06
SCALE = 2.0**-13
LOW_PAIRS = ((0, 0), (0, 1), (1, 1), (0, 2), (1, 2), (2, 2))
TOP_PAIRS = ((0, 3), (1, 3), (2, 3))

F32 = jnp.float32
BF16 = jnp.bfloat16


def routes(count):
    rows = count // GRID
    assert rows % 2 == 0 and GRID == 4
    first, across, second, between = {}, {}, {}, {}
    for s in range(count):
        r, c = divmod(s, GRID)
        over = s + GRID if r % 2 == 0 else s - GRID
        side = s + 1 if c == 1 else s - 1
        across[s] = s + 1 if c % 2 == 0 else s - 1
        if c in (0, GRID - 1):
            first[s] = over
        else:
            first[s], second[s] = side, over
        beyond = s - GRID if r % 2 == 0 else s + GRID
        if 0 <= beyond < count:
            between[s] = beyond
    found = {"first": first, "across": across, "second": second}
    if between:
        found["between"] = between
    return found


def permute(block, route):
    segs, count = lax.axis_size("seg"), lax.axis_size("sec")
    pairs = []
    for g in range(segs):
        for target in range(count):
            if target in route:
                pairs.append((g * count + route[target], g * count + target))
            else:
                pairs.append(((g ^ 1) * count + target, g * count + target))
    return lax.ppermute(block, ("seg", "sec"), pairs)


def reached(route):
    s = lax.axis_index("sec")
    return functools.reduce(jnp.logical_or, [s == t for t in route])


def first_term(route):
    place = {-1: 0, 1: 1, -GRID: 2, GRID: 3}
    s = lax.axis_index("sec")
    start = jnp.int32(0)
    for target, source in route.items():
        start = jnp.where(s == target, W_ZERO + W_HOP * place[source - target], start)
    return start


def split(value):
    high = value.astype(BF16)
    return high, (value - high.astype(F32)).astype(BF16)


def beside(parts):
    return jnp.concatenate(parts, axis=1)


def contract(left, right, block, rest=None, fine=False):
    n, size = left.shape[0], left.shape[1]
    tall = left.reshape(n * size, size)
    inner = jnp.dot(tall, block, preferred_element_type=F32)
    if rest is not None:
        inner = inner + jnp.dot(tall, rest, preferred_element_type=F32)
    pieces = split(inner) if fine else (inner.astype(BF16),)
    a = beside([p[w * size : (w + 1) * size] for p in pieces for w in range(n)])
    b = beside([right[w] for w in range(n)] * len(pieces))
    return lax.dot_general(a, b, (((1,), (1,)), ((), ())), preferred_element_type=F32)


def slot(ref, k):
    return ref[k * W_HOP : (k + 1) * W_HOP]


def row_dot(a, b):
    total = jnp.sum(a * b, axis=0, keepdims=True)
    return sum(total[:, k : k + 128] for k in range(0, total.shape[1], 128))


def start_kernel(psi_hbm, dims_hbm, x_ref, low_ref, mask_ref, psi_ref, dims_ref, sems):
    copies = (
        pltpu.make_async_copy(dims_hbm.at[0], dims_ref, sems.at[0]),
        pltpu.make_async_copy(psi_hbm.at[0, 0], psi_ref, sems.at[1]),
    )
    for c in copies:
        c.start()
    for c in copies:
        c.wait()
    rows = lax.broadcasted_iota(jnp.int32, mask_ref.shape, 0)
    cols = lax.broadcasted_iota(jnp.int32, mask_ref.shape, 1)
    keep = (rows < dims_ref[0, 0]) & (cols < dims_ref[0, 1])
    x = jnp.where(keep, psi_ref[...], 0.0)
    x_ref[...] = x
    low_ref[...] = x.astype(BF16)
    mask_ref[...] = jnp.where(keep, SCALE, 0.0)


def load_kernel(
    ways, left_hbm, right_hbm, low_ref, across_ref, total_ref, left_ref, right_ref, sems
):
    starts = [0] + [first_term(w) for w in ways]
    copies = []
    for k, start in enumerate(starts):
        for side, (hbm, ref) in enumerate(((left_hbm, left_ref), (right_hbm, right_ref))):
            copies.append(
                pltpu.make_async_copy(
                    hbm.at[0, 0, pl.ds(start, W_HOP)],
                    ref.at[pl.ds(k * W_HOP, W_HOP)],
                    sems.at[2 * k + side],
                )
            )
    for c in copies:
        c.start()
    for c in copies[:2]:
        c.wait()
    total = contract(slot(left_ref, 0), slot(right_ref, 0), low_ref[...])
    for c in copies[2:4]:
        c.wait()
    total_ref[...] = total + contract(slot(left_ref, 1), slot(right_ref, 1), across_ref[...])
    for c in copies[4:]:
        c.wait()


def early_kernel(left_ref, right_ref, low_ref, across_ref, out_ref):
    out_ref[...] = contract(slot(left_ref, 0), slot(right_ref, 0), low_ref[...]) + contract(
        slot(left_ref, 1), slot(right_ref, 1), across_ref[...]
    )


def middle_kernel(left_ref, right_ref, total_ref, block_ref, out_ref):
    out_ref[...] = total_ref[...] + contract(
        slot(left_ref, 2), slot(right_ref, 2), block_ref[...]
    )


def image_into(u_ref, ways, left_ref, right_ref, mask_ref, total_ref, blocks):
    u_ref[...] = total_ref[...]
    for k, (way, ref) in enumerate(zip(ways, blocks)):

        @pl.when(reached(way))
        def _():
            u_ref[...] += contract(slot(left_ref, 3 + k), slot(right_ref, 3 + k), ref[...])

    u = u_ref[...] * mask_ref[...]
    u_ref[...] = u
    return u


def late_kernel(ways, packed, left_ref, right_ref, mask_ref, total_ref, *refs):
    n = len(ways)
    if packed:
        before_ref, u_ref, low_ref, pack_ref = refs[n:]
    else:
        u_ref, low_ref = refs[n:]
    u = image_into(u_ref, ways, left_ref, right_ref, mask_ref, total_ref, refs[:n])
    low = u.astype(BF16)
    low_ref[...] = low
    if packed:
        size = u.shape[0]
        pack_ref[:size] = before_ref[...]
        pack_ref[size:] = low


def last_kernel(ways, left_ref, right_ref, mask_ref, total_ref, *refs):
    n = len(ways)
    u0_ref, u1_ref, u2_ref, u_ref, dots_ref = refs[n:]
    u = image_into(u_ref, ways, left_ref, right_ref, mask_ref, total_ref, refs[:n])
    dots_ref[...] = jnp.zeros_like(dots_ref)
    for place, ref in enumerate((u0_ref, u1_ref, u2_ref)):
        dots_ref[place : place + 1] = row_dot(ref[...], u)


def gram_kernel(u0_ref, u1_ref, u2_ref, dots_ref):
    u = [r[...] for r in (u0_ref, u1_ref, u2_ref)]
    dots_ref[...] = jnp.zeros_like(dots_ref)
    for place, (i, j) in enumerate(LOW_PAIRS):
        dots_ref[place : place + 1] = row_dot(u[i], u[j])


def join_kernel(low_ref, top_ref, prior_ref, out_ref):
    out_ref[:8] = low_ref[...]
    out_ref[8:16] = top_ref[...]
    out_ref[16:] = prior_ref[...]


def table_of(sums, low, top=None):
    table = {}
    for first, pairs in ((low, LOW_PAIRS), (top, TOP_PAIRS)):
        if first is not None:
            for place, (i, j) in enumerate(pairs):
                row = sums[first + place : first + place + 1]
                table[i, j] = table[j, i] = jnp.sum(row, axis=(0, 1), keepdims=True)
    return table


def apply(c):
    return [None] + [None if a is None else a * (1.0 / SCALE) for a in c]


def solve(table, entries):
    def dot(c, d):
        out = jnp.zeros((1, 1), F32)
        for i, a in enumerate(c):
            for j, b in enumerate(d):
                if a is not None and b is not None:
                    out = out + a * b * table[i, j]
        return out

    inv = 1.0 / entries
    v0 = [1.0 / jnp.sqrt(table[0, 0] * inv + EPSILON)]
    w = apply(v0)
    alpha0 = dot(w, v0) * inv
    r = [-alpha0 * v0[0], w[1]]
    beta0 = jnp.sqrt(dot(r, r) * inv + EPSILON)
    second = [c / beta0 for c in r]
    w = apply(second)
    alpha1 = dot(w, second) * inv
    r = [-alpha1 * second[0] - beta0 * v0[0], w[1] - alpha1 * second[1], w[2]]
    beta1 = jnp.sqrt(dot(r, r) * inv + EPSILON)
    third = [c / beta1 for c in r]
    values = [alpha0, alpha1, None, beta0, beta1]
    image = apply(third)
    if (0, 3) in table:
        values[2] = dot(image, third) * inv
    return second, third, image, values


def combine(coefs, blocks):
    out = None
    for c, b in zip(coefs, blocks):
        if c is not None:
            out = c * b if out is None else out + c * b
    return out


def end_kernel(
    entries, sums_ref, u0_ref, u1_ref, u2_ref, u3_ref, left_ref, prev01_ref, prev2_ref,
    second_ref, third_ref, image_ref, coef_ref, boundary_ref,
):
    sums = sums_ref[...]
    second, third, image, values = solve(table_of(sums, 0, 8), entries)
    _, prior, _, _ = solve(table_of(sums, 16), entries)
    us = [r[...] for r in (u0_ref, u1_ref, u2_ref, u3_ref)]
    size = us[0].shape[0]
    vector = combine(third, us)
    own = vector.astype(BF16)
    lows = (prev01_ref[:size], prev01_ref[size:], prev2_ref[...])
    before = combine(prior, [v.astype(F32) for v in lows])
    before = jnp.where(lax.axis_index("seg") > 0, before, 0.0).astype(BF16)
    env = jnp.dot(left_ref[0], own, preferred_element_type=F32).astype(BF16)
    dims = (((0,), (0,)), ((), ()))
    total = lax.dot_general(own, env, dims, preferred_element_type=F32)
    total = total + lax.dot_general(before, env, dims, preferred_element_type=F32)
    boundary_ref[0, 0] = total * (1.0 / size**0.5)
    third_ref[0, 0] = vector
    second_ref[0, 0] = combine(second, us)
    image_ref[0, 0] = combine(image, us)
    for place, value in enumerate(values):
        coef_ref[:, place : place + 1] = value


def kernel_call(body, out_shape, n_in, hbm=(), scratch=(), flops=0, moved=0):
    def spec(k):
        return pl.BlockSpec(memory_space=pl.ANY if k in hbm else pltpu.VMEM)

    return pl.pallas_call(
        body,
        out_shape=out_shape,
        in_specs=[spec(k) for k in range(n_in)],
        out_specs=jax.tree.map(lambda _: pl.BlockSpec(memory_space=pltpu.VMEM), out_shape),
        scratch_shapes=scratch,
        compiler_params=pltpu.CompilerParams(vmem_limit_bytes=24 << 20),
        cost_estimate=pl.CostEstimate(flops=flops, bytes_accessed=moved, transcendentals=0),
    )


def body(psi, sector_dims, env_left, env_right):
    size = psi.shape[-1]
    count, segs = lax.axis_size("sec"), lax.axis_size("seg")
    entries = float(count * size * size)

    def block(dtype, rows=size):
        return jax.ShapeDtypeStruct((rows, size), dtype)

    eight = jax.ShapeDtypeStruct((8, 128), F32)
    ways = routes(count)
    late = list(ways)[2:]
    last_ways = [ways[n] for n in late]
    onward = [(g, (g + 1) % segs) for g in range(segs)]
    product = 2 * 2 * size**3 * W_HOP

    def in_hbm(a):
        return pltpu.with_memory_space_constraint(a, pltpu.HBM)

    x, low, mask = kernel_call(
        start_kernel,
        (block(F32), block(BF16), block(F32)),
        2,
        hbm=(0, 1),
        scratch=[
            pltpu.VMEM((size, size), F32),
            pltpu.SMEM((1, 2), jnp.int32),
            pltpu.SemaphoreType.DMA((2,)),
        ],
        moved=2**20,
    )(in_hbm(psi), in_hbm(sector_dims))
    us = [x]
    for step in range(3):
        found = {}
        for n, way in ways.items():
            found[n] = permute(low, way)
        if step == 1:
            prev01 = lax.ppermute(pack, "seg", onward)
        if step == 2:
            dots = kernel_call(gram_kernel, eight, 3)(*us)
            prior = lax.ppermute(dots, "seg", onward)
            prev2 = lax.ppermute(low, "seg", onward)
        if step == 0:
            slots = 1 + len(ways)
            held = pltpu.VMEM((slots * W_HOP, size, size), BF16)
            total, left, right = kernel_call(
                functools.partial(load_kernel, [ways["across"], ways["first"]] + [ways[n] for n in late]),
                (block(F32), held, held),
                4,
                hbm=(0, 1),
                scratch=[pltpu.SemaphoreType.DMA((2 * slots,))],
                flops=2 * product,
                moved=8 << 20,
            )(in_hbm(env_left), in_hbm(env_right), low, found["across"])
        else:
            total = kernel_call(early_kernel, block(F32), 4, flops=2 * product)(
                left, right, low, found["across"]
            )
        total = kernel_call(middle_kernel, block(F32), 4, flops=product)(
            left, right, total, found["first"]
        )
        args = (left, right, mask, total, *[found[n] for n in late])
        n = len(late)
        if step == 0:
            u, low, pack = kernel_call(
                functools.partial(late_kernel, last_ways, True),
                (block(F32), block(BF16), block(BF16, 2 * size)),
                5 + n,
                flops=n * product,
            )(*args, low)
        elif step == 1:
            u, low = kernel_call(
                functools.partial(late_kernel, last_ways, False),
                (block(F32), block(BF16)),
                4 + n,
                flops=n * product,
            )(*args)
        else:
            u, top = kernel_call(
                functools.partial(last_kernel, last_ways),
                (block(F32), eight),
                7 + n,
                flops=n * product,
            )(*args, *us)
        us.append(u)
    sums = kernel_call(join_kernel, jax.ShapeDtypeStruct((24, 128), F32), 3)(dots, top, prior)
    hop = 1
    while hop < count:
        sums = sums + lax.ppermute(sums, "sec", [(i, i ^ hop) for i in range(count)])
        hop *= 2
    full = jax.ShapeDtypeStruct((1, 1, size, size), F32)
    return tuple(
        kernel_call(
            functools.partial(end_kernel, entries),
            (full, full, full, jax.ShapeDtypeStruct((1, 5), F32), full),
            8,
            flops=6 * size**3,
        )(sums, *us, left, prev01, prev2)
    )


def solution(mesh):
    count = mesh.shape["sec"]
    assert count & (count - 1) == 0
    in_specs = (
        P("seg", "sec", None, None),
        P("seg", "sec", None),
        P("seg", "sec", None, None, None),
        P("seg", "sec", None, None, None),
    )
    out_specs = (
        P("seg", "sec", None, None),
        P("seg", "sec", None, None),
        P("seg", "sec", None, None),
        P("seg", None),
        P("seg", "sec", None, None),
    )
    return jax.shard_map(body, mesh=mesh, in_specs=in_specs, out_specs=out_specs, check_vma=False)
```

time: 161 us -> 49.6 us (0.31)
  blocking collectives: 62.6 us -> 0 us
  matrix products: 38.1 us -> 0 us
  waiting for transfers between devices: 0.03 us -> 22.3 us
  starting transfers between devices: 36.6 us -> 15.4 us
  between operations: 15.9 us -> 0.72 us
  Pallas kernels: 0 us -> 11.1 us
  other arithmetic: 4.15 us -> 0.01 us
  local copies, waits for them, and re-layouts: 1.93 us -> 0 us
    psum x4 -> x0, blocking collectives: 62.6 us -> none  [the longest x3 43.9 us: body(): lax.psum((jnp.sum(image * image), jnp.sum(image * current), jnp.sum(image...]
    dot_general x18 -> x0, matrix products: 38.1 us -> none  [the longest x15 35.9 us: contract(): jnp.einsum('wik,wlk->il', inner, right_env[start:stop], preferred_element...]
    ppermute x13 -> x15, waiting for transfers between devices: 0.03 us -> 22.3 us  [the longest x9 11.9 us: permute(): return lax.ppermute(block, ('seg', 'sec'), pairs)]
    ppermute x13 -> x15, starting transfers between devices: 36.6 us -> 15.4 us  [the longest x9 11.6 us: permute(): return lax.ppermute(block, ('seg', 'sec'), pairs)]
    pallas_call x0 -> x13, Pallas kernels: none -> 11.1 us  [the longest x1 3.12 us: body(): kernel_call(functools.partial(load_kernel, [ways['across'], ways['first']...]
    reduce_sum x1 -> x0, other arithmetic: 1.7 us -> none  [body(): squared_start = lax.psum(jnp.sum(start_vec * start_vec), 'sec')]
  transfers between devices with their start and end apart: 13 -> 15, of which waited for: 0 -> 8; matrix products, arithmetic and copies ran while one was open for 20% -> 0% of each run, Pallas kernels for 0% -> 17%
where the time goes in v2:
time: 49.6 us; the launch traced here: 49.4 us
  waiting for transfers between devices  22.3 us (45%)
  starting transfers between devices  15.4 us (31%)
  Pallas kernels  11.1 us (22%)
  between operations  0.72 us (1%)
    ppermute x9, waiting for transfers between devices, permute(): return lax.ppermute(block, ('seg', 'sec'), pairs)  11.9 us
    ppermute x9, starting transfers between devices, permute(): return lax.ppermute(block, ('seg', 'sec'), pairs)  11.6 us
    ppermute x3, waiting for transfers between devices, body(): lax.ppermute(sums, 'sec', [(i, i ^ hop) for i in range(count)])  9.27 us
    pallas_call x1, Pallas kernels, body(): kernel_call(functools.partial(load_kernel, [ways['across'], ways['first']...  3.12 us
    pallas_call x2, Pallas kernels, body(): kernel_call(early_kernel, block(F32), 4, flops=2 * product)  2.94 us
    pallas_call x3, Pallas kernels, body(): kernel_call(middle_kernel, block(F32), 4, flops=product)  2.02 us
    ppermute x1, starting transfers between devices, body(): prev01 = lax.ppermute(pack, 'seg', onward)  1.87 us
    pallas_call x1, Pallas kernels, body(): kernel_call(functools.partial(end_kernel, entries), (full, full, full, ja...  1.5 us
  transfers between devices with their start and end apart: 15, of which 8 were waited for; matrix products, arithmetic and copies ran while one was open for 0% of the time, Pallas kernels for 17%

profile of v2, /device:TPU:0, one launch (start us, length us, event | category | flops | bytes accessed | tf_op | source)
XLA Modules:
  0.0 49.4 jit_solution(4232629677619833875)
XLA Ops:
  0.6 1.0 %shard_map.83 = (f32[256,256]{1,0:T(8,128)S(1)}, bf16[256,256]{1,0:T(8,128)(2,1)S(1)}, f32[256,256]{1,0:T(8,128)S(1)}) custom-call(f32[1,1,256,256]{3,2,1,0:T(8,128)} %psi_hbm.1, s32[1,1,2]{2,1,0:T(1,128)} %dims_hbm.1), custom_call_target="tpu_custom_call" | custom-call | bytes 1048576 | tf_op jit(solution)/shard_map/pallas_call | solution.py:316
  1.7 0.6 %collective-permute-start = (bf16[256,256]{1,0:T(8,128)(2,1)S(1)}, bf16[256,256]{1,0:T(8,128)(2,1)S(1)}, u32[]{:S(2)}, u32[]{:S(2)}) collective-permute-start(bf16[256,256]{1,0:T(8,128)(2,1)S(1)} %get-tuple-element.19.low_ref.refs_1_), channel_id=1, source_target_pairs={{1,0},{0,1},{3,2},{2,3},{5,4},{4,5},{7,6},{6,7},{9,8},{8,9},{11,10... | collective-permute-start | bytes 393224 | tf_op jit(solution)/shard_map/ppermute | solution.py:54
  2.2 3.6 %collective-permute-start.1 = (bf16[256,256]{1,0:T(8,128)(2,1)S(1)}, bf16[256,256]{1,0:T(8,128)(2,1)S(1)}, u32[]{:S(2)}, u32[]{:S(2)}) collective-permute-start(bf16[256,256]{1,0:T(8,128)(2,1)S(1)} %get-tuple-element.19.low_ref.refs_1_), channel_id=1, source_target_pairs={{4,0},{2,1},{1,2},{7,3},{0,4},{6,5},{5,6},{3,7},{12,8},{10,9},{9,1... | collective-permute-start | bytes 393224 | tf_op jit(solution)/shard_map/ppermute | solution.py:54
  5.9 1.5 %collective-permute-start.2 = (bf16[256,256]{1,0:T(8,128)(2,1)S(1)}, bf16[256,256]{1,0:T(8,128)(2,1)S(1)}, u32[]{:S(2)}, u32[]{:S(2)}) collective-permute-start(bf16[256,256]{1,0:T(8,128)(2,1)S(1)} %get-tuple-element.19.low_ref.refs_1_), channel_id=1, source_target_pairs={{8,0},{5,1},{6,2},{11,3},{12,4},{1,5},{2,6},{15,7},{0,8},{13,9},{1... | collective-permute-start | bytes 393224 | tf_op jit(solution)/shard_map/ppermute | solution.py:54
  7.4 0.0 collective-permute-done.across_ref
  7.4 3.1 %shard_map.84 = (f32[256,256]{1,0:T(8,128)S(1)}, bf16[24,256,256]{2,1,0:T(8,128)(2,1)S(1)}, bf16[24,256,256]{2,1,0:T(8,128)(2,1)S(1)}) custom-call(bf16[1,1,30,256,256]{4,3,2,1,0:T(8,128)(2,1)} %left_hbm.1, bf16[1,1,30,256,256]{4,3,2,1,0:T(8,128)(2,1)} %right_hbm.1, bf16[256,256]{1,0:T(8,128)(2,1)S(1)} %get-tuple-element.19.low_ref.refs_1_, ...), custom_call_target="tpu_custom_call" | custom-call | flops 805306368 | bytes 8388608 | tf_op jit(solution)/shard_map/pallas_call | solution.py:342
  10.5 0.2 collective-permute-done.1.block_ref
  10.7 0.7 %shard_map.85.total_ref = f32[256,256]{1,0:T(8,128)S(1)} custom-call(bf16[24,256,256]{2,1,0:T(8,128)(2,1)S(1)} %get-tuple-element.20.left_ref, bf16[24,256,256]{2,1,0:T(8,128)(2,1)S(1)} %get-tuple-element.21.right_ref, f32[256,256]{1,0:T(8,128)S(1)} %get-tuple-element.23.total_ref, bf16[256,256]{1,0:T(8,128)(2,1)S(1)} %collective-permute-done.1.block_ref), custom_call_target="tpu_custom_call" | custom-call | flops 402653184 | tf_op jit(solution)/shard_map/pallas_call | solution.py:355
  11.4 0.0 collective-permute-done.2.refs_0_
  11.4 0.1 shard_map.86
  11.5 2.2 %collective-permute-start.3 = (bf16[256,256]{1,0:T(8,128)(2,1)S(1)}, bf16[256,256]{1,0:T(8,128)(2,1)S(1)}, u32[]{:S(2)}, u32[]{:S(2)}) collective-permute-start(bf16[256,256]{1,0:T(8,128)(2,1)S(1)} %get-tuple-element.25.low_ref), channel_id=1, source_target_pairs={{1,0},{0,1},{3,2},{2,3},{5,4},{4,5},{7,6},{6,7},{9,8},{8,9},{11,10... | collective-permute-start | bytes 393224 | tf_op jit(solution)/shard_map/ppermute | solution.py:54
  13.7 0.2 collective-permute-start.4
  13.9 1.6 %collective-permute-start.5 = (bf16[256,256]{1,0:T(8,128)(2,1)S(1)}, bf16[256,256]{1,0:T(8,128)(2,1)S(1)}, u32[]{:S(2)}, u32[]{:S(2)}) collective-permute-start(bf16[256,256]{1,0:T(8,128)(2,1)S(1)} %get-tuple-element.25.low_ref), channel_id=1, source_target_pairs={{8,0},{5,1},{6,2},{11,3},{12,4},{1,5},{2,6},{15,7},{0,8},{13,9},{1... | collective-permute-start | bytes 393224 | tf_op jit(solution)/shard_map/ppermute | solution.py:54
  15.5 0.0 collective-permute-done.3.across_ref
  15.5 1.5 %shard_map.87.total_ref = f32[256,256]{1,0:T(8,128)S(1)} custom-call(bf16[24,256,256]{2,1,0:T(8,128)(2,1)S(1)} %get-tuple-element.20.left_ref, bf16[24,256,256]{2,1,0:T(8,128)(2,1)S(1)} %get-tuple-element.21.right_ref, bf16[256,256]{1,0:T(8,128)(2,1)S(1)} %get-tuple-element.25.low_ref, bf16[256,256]{1,0:T(8,128)(2,1)S(1)} %collective-permute-done.3.across_ref), custom_call_target="tpu_custom_call" | custom-call | flops 805306368 | tf_op jit(solution)/shard_map/pallas_call | solution.py:352
  17.0 6.2 %collective-permute-done.4.block_ref = bf16[256,256]{1,0:T(8,128)(2,1)S(1)} collective-permute-done((bf16[256,256]{1,0:T(8,128)(2,1)S(1)}, bf16[256,256]{1,0:T(8,128)(2,1)S(1)}, u32[]{:S(2)}, u32[]{:S(2)}) %collective-permute-start.4) | collective-permute-done | bytes 131104 | tf_op jit(solution)/shard_map/ppermute | solution.py:54
  23.2 0.7 %shard_map.88.total_ref = f32[256,256]{1,0:T(8,128)S(1)} custom-call(bf16[24,256,256]{2,1,0:T(8,128)(2,1)S(1)} %get-tuple-element.20.left_ref, bf16[24,256,256]{2,1,0:T(8,128)(2,1)S(1)} %get-tuple-element.21.right_ref, f32[256,256]{1,0:T(8,128)S(1)} %shard_map.87.total_ref, bf16[256,256]{1,0:T(8,128)(2,1)S(1)} %collective-permute-done.4.block_ref), custom_call_target="tpu_custom_call" | custom-call | flops 402653184 | tf_op jit(solution)/shard_map/pallas_call | solution.py:355
  23.9 0.0 collective-permute-done.5.refs_0_
  23.9 0.1 shard_map.89
  24.0 0.4 collective-permute-start.6
  24.4 1.9 %collective-permute-start.13 = (bf16[512,256]{1,0:T(8,128)(2,1)S(1)}, bf16[512,256]{1,0:T(8,128)(2,1)S(1)}, u32[]{:S(2)}, u32[]{:S(2)}) collective-permute-start(bf16[512,256]{1,0:T(8,128)(2,1)S(1)} %get-tuple-element.30), channel_id=1, source_target_pairs={{0,8},{8,16},{16,24},{24,0},{1,9},{9,17},{17,25},{25,1},{2,10},{10... | collective-permute-start | bytes 786440 | tf_op jit(solution)/shard_map/ppermute | solution.py:334
  26.3 0.0 collective-permute-start.7
  26.3 1.5 %collective-permute-start.8 = (bf16[256,256]{1,0:T(8,128)(2,1)S(1)}, bf16[256,256]{1,0:T(8,128)(2,1)S(1)}, u32[]{:S(2)}, u32[]{:S(2)}) collective-permute-start(bf16[256,256]{1,0:T(8,128)(2,1)S(1)} %get-tuple-element.27.low_ref), channel_id=1, source_target_pairs={{8,0},{5,1},{6,2},{11,3},{12,4},{1,5},{2,6},{15,7},{0,8},{13,9},{1... | collective-permute-start | bytes 393224 | tf_op jit(solution)/shard_map/ppermute | solution.py:54
  27.8 0.5 %collective-permute-start.14 = (bf16[256,256]{1,0:T(8,128)(2,1)S(1)}, bf16[256,256]{1,0:T(8,128)(2,1)S(1)}, u32[]{:S(2)}, u32[]{:S(2)}) collective-permute-start(bf16[256,256]{1,0:T(8,128)(2,1)S(1)} %get-tuple-element.27.low_ref), channel_id=1, source_target_pairs={{0,8},{8,16},{16,24},{24,0},{1,9},{9,17},{17,25},{25,1},{2,10},{10... | collective-permute-start | bytes 393224 | tf_op jit(solution)/shard_map/ppermute | solution.py:338
  28.3 0.2 shard_map.90.low_ref
  28.5 0.0 collective-permute-done.6.across_ref
  28.5 1.1 %collective-permute-start.9 = (f32[8,128]{1,0:T(8,128)S(1)}, f32[8,128]{1,0:T(8,128)S(1)}, u32[]{:S(2)}, u32[]{:S(2)}) collective-permute-start(f32[8,128]{1,0:T(8,128)S(1)} %shard_map.90.low_ref), channel_id=1, source_target_pairs={{0,8},{8,16},{16,24},{24,0},{1,9},{9,17},{17,25},{25,1},{2,10},{10... | collective-permute-start | bytes 12296 | tf_op jit(solution)/shard_map/ppermute | solution.py:337
  29.6 1.5 %shard_map.91.total_ref = f32[256,256]{1,0:T(8,128)S(1)} custom-call(bf16[24,256,256]{2,1,0:T(8,128)(2,1)S(1)} %get-tuple-element.20.left_ref, bf16[24,256,256]{2,1,0:T(8,128)(2,1)S(1)} %get-tuple-element.21.right_ref, bf16[256,256]{1,0:T(8,128)(2,1)S(1)} %get-tuple-element.27.low_ref, bf16[256,256]{1,0:T(8,128)(2,1)S(1)} %collective-permute-done.6.across_ref), custom_call_target="tpu_custom_call" | custom-call | flops 805306368 | tf_op jit(solution)/shard_map/pallas_call | solution.py:352
  31.1 3.9 %collective-permute-done.7.block_ref = bf16[256,256]{1,0:T(8,128)(2,1)S(1)} collective-permute-done((bf16[256,256]{1,0:T(8,128)(2,1)S(1)}, bf16[256,256]{1,0:T(8,128)(2,1)S(1)}, u32[]{:S(2)}, u32[]{:S(2)}) %collective-permute-start.7) | collective-permute-done | bytes 131104 | tf_op jit(solution)/shard_map/ppermute | solution.py:54
  35.0 0.7 %shard_map.92.total_ref = f32[256,256]{1,0:T(8,128)S(1)} custom-call(bf16[24,256,256]{2,1,0:T(8,128)(2,1)S(1)} %get-tuple-element.20.left_ref, bf16[24,256,256]{2,1,0:T(8,128)(2,1)S(1)} %get-tuple-element.21.right_ref, f32[256,256]{1,0:T(8,128)S(1)} %shard_map.91.total_ref, bf16[256,256]{1,0:T(8,128)(2,1)S(1)} %collective-permute-done.7.block_ref), custom_call_target="tpu_custom_call" | custom-call | flops 402653184 | tf_op jit(solution)/shard_map/pallas_call | solution.py:355
  35.7 1.6 %collective-permute-done.8.refs_0_ = bf16[256,256]{1,0:T(8,128)(2,1)S(1)} collective-permute-done((bf16[256,256]{1,0:T(8,128)(2,1)S(1)}, bf16[256,256]{1,0:T(8,128)(2,1)S(1)}, u32[]{:S(2)}, u32[]{:S(2)}) %collective-permute-start.8) | collective-permute-done | bytes 131104 | tf_op jit(solution)/shard_map/ppermute | solution.py:54
  37.2 0.1 shard_map.93
  37.4 1.1 %collective-permute-done.9.prior_ref = f32[8,128]{1,0:T(8,128)S(1)} collective-permute-done((f32[8,128]{1,0:T(8,128)S(1)}, f32[8,128]{1,0:T(8,128)S(1)}, u32[]{:S(2)}, u32[]{:S(2)}) %collective-permute-start.9) | collective-permute-done | bytes 4128 | tf_op jit(solution)/shard_map/ppermute | solution.py:337
  38.4 0.0 collective-permute-start.10
  38.4 1.2 %collective-permute-done.10 = f32[24,128]{1,0:T(8,128)S(1)} collective-permute-done((f32[24,128]{1,0:T(8,128)S(1)}, f32[24,128]{1,0:T(8,128)S(1)}, u32[]{:S(2)}, u32[]{:S(2)}) %collective-permute-start.10) | collective-permute-done | bytes 12320 | tf_op jit(solution)/shard_map/ppermute | solution.py:385
  39.6 0.0 collective-permute-start.11
  39.6 3.7 %collective-permute-done.11 = f32[24,128]{1,0:T(8,128)S(1)} collective-permute-done((f32[24,128]{1,0:T(8,128)S(1)}, f32[24,128]{1,0:T(8,128)S(1)}, u32[]{:S(2)}, u32[]{:S(2)}) %collective-permute-start.11) | collective-permute-done | bytes 12320 | tf_op jit(solution)/shard_map/ppermute | solution.py:385
  43.3 0.2 collective-permute-start.12
  43.5 4.4 %collective-permute-done.12 = f32[24,128]{1,0:T(8,128)S(1)} collective-permute-done((f32[24,128]{1,0:T(8,128)S(1)}, f32[24,128]{1,0:T(8,128)S(1)}, u32[]{:S(2)}, u32[]{:S(2)}) %collective-permute-start.12) | collective-permute-done | bytes 12320 | tf_op jit(solution)/shard_map/ppermute | solution.py:385
  47.9 0.0 collective-permute-done.14.prev2_ref
  47.9 0.0 collective-permute-done.13.prev01_ref
  47.9 1.5 %shard_map.95 = (f32[1,1,256,256]{3,2,1,0:T(8,128)}, f32[1,1,256,256]{3,2,1,0:T(8,128)}, f32[1,1,256,256]{3,2,1,0:T(8,128)}, f32[1,5]{1,0:T(1,128)}, f32[1,1,256,256]{3,2,1,0:T(8,128)}) custom-call(f32[24,128]{1,0:T(8,128)S(1)} %add.11.sums_ref, f32[256,256]{1,0:T(8,128)S(1)} %get-tuple-element.18.u0_ref.refs_1_, ...), custom_call_target="tpu_custom_call" | custom-call | flops 100663296 | tf_op jit(solution)/shard_map/pallas_call | solution.py:389
  (4 shorter events, 0.0 us)
Async XLA Ops:
  1.7 5.7 %collective-permute-start = (bf16[256,256]{1,0:T(8,128)(2,1)S(1)}, bf16[256,256]{1,0:T(8,128)(2,1)S(1)}, u32[]{:S(2)}, u32[]{:S(2)}) collective-permute-start(bf16[256,256]{1,0:T(8,128)(2,1)S(1)} %get-tuple-element.19.low_ref.refs_1_), channel_id=1, source_target_pairs={{1,0},{0,1},{3,2},{2,3},{5,4},{4,5},{7,6},{6,7},{9,8},{8,9},{11,10... | collective-permute-start | bytes 393224 | tf_op jit(solution)/shard_map/ppermute | solution.py:54
  2.2 8.5 %collective-permute-start.1 = (bf16[256,256]{1,0:T(8,128)(2,1)S(1)}, bf16[256,256]{1,0:T(8,128)(2,1)S(1)}, u32[]{:S(2)}, u32[]{:S(2)}) collective-permute-start(bf16[256,256]{1,0:T(8,128)(2,1)S(1)} %get-tuple-element.19.low_ref.refs_1_), channel_id=1, source_target_pairs={{4,0},{2,1},{1,2},{7,3},{0,4},{6,5},{5,6},{3,7},{12,8},{10,9},{9,1... | collective-permute-start | bytes 393224 | tf_op jit(solution)/shard_map/ppermute | solution.py:54
  5.9 5.5 %collective-permute-start.2 = (bf16[256,256]{1,0:T(8,128)(2,1)S(1)}, bf16[256,256]{1,0:T(8,128)(2,1)S(1)}, u32[]{:S(2)}, u32[]{:S(2)}) collective-permute-start(bf16[256,256]{1,0:T(8,128)(2,1)S(1)} %get-tuple-element.19.low_ref.refs_1_), channel_id=1, source_target_pairs={{8,0},{5,1},{6,2},{11,3},{12,4},{1,5},{2,6},{15,7},{0,8},{13,9},{1... | collective-permute-start | bytes 393224 | tf_op jit(solution)/shard_map/ppermute | solution.py:54
  11.5 4.0 %collective-permute-start.3 = (bf16[256,256]{1,0:T(8,128)(2,1)S(1)}, bf16[256,256]{1,0:T(8,128)(2,1)S(1)}, u32[]{:S(2)}, u32[]{:S(2)}) collective-permute-start(bf16[256,256]{1,0:T(8,128)(2,1)S(1)} %get-tuple-element.25.low_ref), channel_id=1, source_target_pairs={{1,0},{0,1},{3,2},{2,3},{5,4},{4,5},{7,6},{6,7},{9,8},{8,9},{11,10... | collective-permute-start | bytes 393224 | tf_op jit(solution)/shard_map/ppermute | solution.py:54
  13.7 9.5 %collective-permute-start.4 = (bf16[256,256]{1,0:T(8,128)(2,1)S(1)}, bf16[256,256]{1,0:T(8,128)(2,1)S(1)}, u32[]{:S(2)}, u32[]{:S(2)}) collective-permute-start(bf16[256,256]{1,0:T(8,128)(2,1)S(1)} %get-tuple-element.25.low_ref), channel_id=1, source_target_pairs={{4,0},{2,1},{1,2},{7,3},{0,4},{6,5},{5,6},{3,7},{12,8},{10,9},{9,1... | collective-permute-start | bytes 393224 | tf_op jit(solution)/shard_map/ppermute | solution.py:54
  13.9 10.0 %collective-permute-start.5 = (bf16[256,256]{1,0:T(8,128)(2,1)S(1)}, bf16[256,256]{1,0:T(8,128)(2,1)S(1)}, u32[]{:S(2)}, u32[]{:S(2)}) collective-permute-start(bf16[256,256]{1,0:T(8,128)(2,1)S(1)} %get-tuple-element.25.low_ref), channel_id=1, source_target_pairs={{8,0},{5,1},{6,2},{11,3},{12,4},{1,5},{2,6},{15,7},{0,8},{13,9},{1... | collective-permute-start | bytes 393224 | tf_op jit(solution)/shard_map/ppermute | solution.py:54
  24.0 4.5 %collective-permute-start.6 = (bf16[256,256]{1,0:T(8,128)(2,1)S(1)}, bf16[256,256]{1,0:T(8,128)(2,1)S(1)}, u32[]{:S(2)}, u32[]{:S(2)}) collective-permute-start(bf16[256,256]{1,0:T(8,128)(2,1)S(1)} %get-tuple-element.27.low_ref), channel_id=1, source_target_pairs={{1,0},{0,1},{3,2},{2,3},{5,4},{4,5},{7,6},{6,7},{9,8},{8,9},{11,10... | collective-permute-start | bytes 393224 | tf_op jit(solution)/shard_map/ppermute | solution.py:54
  24.4 23.5 %collective-permute-start.13 = (bf16[512,256]{1,0:T(8,128)(2,1)S(1)}, bf16[512,256]{1,0:T(8,128)(2,1)S(1)}, u32[]{:S(2)}, u32[]{:S(2)}) collective-permute-start(bf16[512,256]{1,0:T(8,128)(2,1)S(1)} %get-tuple-element.30), channel_id=1, source_target_pairs={{0,8},{8,16},{16,24},{24,0},{1,9},{9,17},{17,25},{25,1},{2,10},{10... | collective-permute-start | bytes 786440 | tf_op jit(solution)/shard_map/ppermute | solution.py:334
  26.3 8.7 %collective-permute-start.7 = (bf16[256,256]{1,0:T(8,128)(2,1)S(1)}, bf16[256,256]{1,0:T(8,128)(2,1)S(1)}, u32[]{:S(2)}, u32[]{:S(2)}) collective-permute-start(bf16[256,256]{1,0:T(8,128)(2,1)S(1)} %get-tuple-element.27.low_ref), channel_id=1, source_target_pairs={{4,0},{2,1},{1,2},{7,3},{0,4},{6,5},{5,6},{3,7},{12,8},{10,9},{9,1... | collective-permute-start | bytes 393224 | tf_op jit(solution)/shard_map/ppermute | solution.py:54
  26.3 10.9 %collective-permute-start.8 = (bf16[256,256]{1,0:T(8,128)(2,1)S(1)}, bf16[256,256]{1,0:T(8,128)(2,1)S(1)}, u32[]{:S(2)}, u32[]{:S(2)}) collective-permute-start(bf16[256,256]{1,0:T(8,128)(2,1)S(1)} %get-tuple-element.27.low_ref), channel_id=1, source_target_pairs={{8,0},{5,1},{6,2},{11,3},{12,4},{1,5},{2,6},{15,7},{0,8},{13,9},{1... | collective-permute-start | bytes 393224 | tf_op jit(solution)/shard_map/ppermute | solution.py:54
  27.8 20.1 %collective-permute-start.14 = (bf16[256,256]{1,0:T(8,128)(2,1)S(1)}, bf16[256,256]{1,0:T(8,128)(2,1)S(1)}, u32[]{:S(2)}, u32[]{:S(2)}) collective-permute-start(bf16[256,256]{1,0:T(8,128)(2,1)S(1)} %get-tuple-element.27.low_ref), channel_id=1, source_target_pairs={{0,8},{8,16},{16,24},{24,0},{1,9},{9,17},{17,25},{25,1},{2,10},{10... | collective-permute-start | bytes 393224 | tf_op jit(solution)/shard_map/ppermute | solution.py:338
  28.5 9.9 %collective-permute-start.9 = (f32[8,128]{1,0:T(8,128)S(1)}, f32[8,128]{1,0:T(8,128)S(1)}, u32[]{:S(2)}, u32[]{:S(2)}) collective-permute-start(f32[8,128]{1,0:T(8,128)S(1)} %shard_map.90.low_ref), channel_id=1, source_target_pairs={{0,8},{8,16},{16,24},{24,0},{1,9},{9,17},{17,25},{25,1},{2,10},{10... | collective-permute-start | bytes 12296 | tf_op jit(solution)/shard_map/ppermute | solution.py:337
  38.4 1.2 %collective-permute-start.10 = (f32[24,128]{1,0:T(8,128)S(1)}, f32[24,128]{1,0:T(8,128)S(1)}, u32[]{:S(2)}, u32[]{:S(2)}) collective-permute-start(f32[24,128]{1,0:T(8,128)S(1)} %shard_map.94), channel_id=1, source_target_pairs={{0,1},{1,0},{2,3},{3,2},{4,5},{5,4},{6,7},{7,6},{8,9},{9,8},{10,11... | collective-permute-start | bytes 36872 | tf_op jit(solution)/shard_map/ppermute | solution.py:385
  39.6 3.7 %collective-permute-start.11 = (f32[24,128]{1,0:T(8,128)S(1)}, f32[24,128]{1,0:T(8,128)S(1)}, u32[]{:S(2)}, u32[]{:S(2)}) collective-permute-start(f32[24,128]{1,0:T(8,128)S(1)} %add.9), channel_id=1, source_target_pairs={{0,2},{1,3},{2,0},{3,1},{4,6},{5,7},{6,4},{7,5},{8,10},{9,11},{10,... | collective-permute-start | bytes 36872 | tf_op jit(solution)/shard_map/ppermute | solution.py:385
  43.3 4.6 %collective-permute-start.12 = (f32[24,128]{1,0:T(8,128)S(1)}, f32[24,128]{1,0:T(8,128)S(1)}, u32[]{:S(2)}, u32[]{:S(2)}) collective-permute-start(f32[24,128]{1,0:T(8,128)S(1)} %add.10), channel_id=1, source_target_pairs={{0,4},{1,5},{2,6},{3,7},{4,0},{5,1},{6,2},{7,3},{8,12},{9,13},{10,... | collective-permute-start | bytes 36872 | tf_op jit(solution)/shard_map/ppermute | solution.py:385

commit v3 on v2

--- a/solution.py
+++ b/solution.py
@@ -12,6 +12,7 @@
 W_HOP = 6
 GRID = 4
 EPSILON = 1e-06
+PARTS = 2
 SCALE = 2.0**-13
 LOW_PAIRS = ((0, 0), (0, 1), (1, 1), (0, 2), (1, 2), (2, 2))
 TOP_PAIRS = ((0, 3), (1, 3), (2, 3))
@@ -99,21 +100,27 @@
 
 
 def start_kernel(psi_hbm, dims_hbm, x_ref, low_ref, mask_ref, psi_ref, dims_ref, sems):
-    copies = (
-        pltpu.make_async_copy(dims_hbm.at[0], dims_ref, sems.at[0]),
-        pltpu.make_async_copy(psi_hbm.at[0, 0], psi_ref, sems.at[1]),
-    )
+    tall = psi_ref.shape[0] // PARTS
+    copies = [pltpu.make_async_copy(dims_hbm.at[0], dims_ref, sems.at[0])]
+    for k in range(PARTS):
+        part = pl.ds(k * tall, tall)
+        copies.append(
+            pltpu.make_async_copy(psi_hbm.at[0, 0, part], psi_ref.at[part], sems.at[1 + k])
+        )
     for c in copies:
         c.start()
-    for c in copies:
-        c.wait()
-    rows = lax.broadcasted_iota(jnp.int32, mask_ref.shape, 0)
-    cols = lax.broadcasted_iota(jnp.int32, mask_ref.shape, 1)
-    keep = (rows < dims_ref[0, 0]) & (cols < dims_ref[0, 1])
-    x = jnp.where(keep, psi_ref[...], 0.0)
-    x_ref[...] = x
-    low_ref[...] = x.astype(BF16)
-    mask_ref[...] = jnp.where(keep, SCALE, 0.0)
+    copies[0].wait()
+    cols = lax.broadcasted_iota(jnp.int32, (tall, psi_ref.shape[1]), 1)
+    live = cols < dims_ref[0, 1]
+    for k in range(PARTS):
+        part = pl.ds(k * tall, tall)
+        rows = k * tall + lax.broadcasted_iota(jnp.int32, live.shape, 0)
+        keep = live & (rows < dims_ref[0, 0])
+        mask_ref[part] = jnp.where(keep, SCALE, 0.0)
+        copies[1 + k].wait()
+        x = jnp.where(keep, psi_ref[part], 0.0)
+        x_ref[part] = x
+        low_ref[part] = x.astype(BF16)
 
 
 def load_kernel(
@@ -154,17 +161,35 @@
     )
 
 
-def image_into(u_ref, ways, left_ref, right_ref, mask_ref, total_ref, blocks):
-    u_ref[...] = total_ref[...]
-    for k, (way, ref) in enumerate(zip(ways, blocks)):
+def image_into(u_ref, low_ref, ways, left_ref, right_ref, mask_ref, total_ref, blocks):
+    def part(k):
+        return contract(slot(left_ref, 3 + k), slot(right_ref, 3 + k), blocks[k][...])
+
+    def finish(total):
+        u = total * mask_ref[...]
+        u_ref[...] = u
+        if low_ref is not None:
+            low_ref[...] = u.astype(BF16)
+
+    so_far = total_ref
+    for k, way in enumerate(ways[:-1]):
+        if k == 0:
+            u_ref[...] = total_ref[...]
+            so_far = u_ref
 
         @pl.when(reached(way))
         def _():
-            u_ref[...] += contract(slot(left_ref, 3 + k), slot(right_ref, 3 + k), ref[...])
-
-    u = u_ref[...] * mask_ref[...]
-    u_ref[...] = u
-    return u
+            u_ref[...] += part(k)
+
+    here = reached(ways[-1])
+
+    @pl.when(here)
+    def _():
+        finish(so_far[...] + part(len(ways) - 1))
+
+    @pl.when(jnp.logical_not(here))
+    def _():
+        finish(so_far[...])
 
 
 def late_kernel(ways, packed, left_ref, right_ref, mask_ref, total_ref, *refs):
@@ -173,19 +198,18 @@
         before_ref, u_ref, low_ref, pack_ref = refs[n:]
     else:
         u_ref, low_ref = refs[n:]
-    u = image_into(u_ref, ways, left_ref, right_ref, mask_ref, total_ref, refs[:n])
-    low = u.astype(BF16)
-    low_ref[...] = low
+    image_into(u_ref, low_ref, ways, left_ref, right_ref, mask_ref, total_ref, refs[:n])
     if packed:
-        size = u.shape[0]
+        size = low_ref.shape[0]
         pack_ref[:size] = before_ref[...]
-        pack_ref[size:] = low
+        pack_ref[size:] = low_ref[...]
 
 
 def last_kernel(ways, left_ref, right_ref, mask_ref, total_ref, *refs):
     n = len(ways)
     u0_ref, u1_ref, u2_ref, u_ref, dots_ref = refs[n:]
-    u = image_into(u_ref, ways, left_ref, right_ref, mask_ref, total_ref, refs[:n])
+    image_into(u_ref, None, ways, left_ref, right_ref, mask_ref, total_ref, refs[:n])
+    u = u_ref[...]
     dots_ref[...] = jnp.zeros_like(dots_ref)
     for place, ref in enumerate((u0_ref, u1_ref, u2_ref)):
         dots_ref[place : place + 1] = row_dot(ref[...], u)
@@ -321,7 +345,7 @@
         scratch=[
             pltpu.VMEM((size, size), F32),
             pltpu.SMEM((1, 2), jnp.int32),
-            pltpu.SemaphoreType.DMA((2,)),
+            pltpu.SemaphoreType.DMA((1 + PARTS,)),
         ],
         moved=2**20,
     )(in_hbm(psi), in_hbm(sector_dims))

time: 49.6 us -> 49.5 us (level)
  no operation moved by 1% of the time
where the time goes in v3:
time: 49.5 us; the launch traced here: 49.3 us
  waiting for transfers between devices  22.3 us (45%)
  starting transfers between devices  15.3 us (31%)
  Pallas kernels  11 us (22%)
  between operations  0.72 us (1%)
    ppermute x9, waiting for transfers between devices, permute(): return lax.ppermute(block, ('seg', 'sec'), pairs)  11.9 us
    ppermute x9, starting transfers between devices, permute(): return lax.ppermute(block, ('seg', 'sec'), pairs)  11.5 us
    ppermute x3, waiting for transfers between devices, body(): lax.ppermute(sums, 'sec', [(i, i ^ hop) for i in range(count)])  9.32 us
    pallas_call x1, Pallas kernels, body(): kernel_call(functools.partial(load_kernel, [ways['across'], ways['first']...  3.12 us
    pallas_call x2, Pallas kernels, body(): kernel_call(early_kernel, block(F32), 4, flops=2 * product)  2.94 us
    pallas_call x3, Pallas kernels, body(): kernel_call(middle_kernel, block(F32), 4, flops=product)  2.03 us
    ppermute x1, starting transfers between devices, body(): prev01 = lax.ppermute(pack, 'seg', onward)  1.89 us
    pallas_call x1, Pallas kernels, body(): kernel_call(functools.partial(end_kernel, entries), (full, full, full, ja...  1.5 us
  transfers between devices with their start and end apart: 15, of which 8 were waited for; matrix products, arithmetic and copies ran while one was open for 0% of the time, Pallas kernels for 17%

profile of v3, /device:TPU:0, one launch (start us, length us, event | category | flops | bytes accessed | tf_op | source)
XLA Modules:
  0.0 49.3 jit_solution(5488110903625813889)
XLA Ops:
  0.6 1.0 %shard_map.83 = (f32[256,256]{1,0:T(8,128)S(1)}, bf16[256,256]{1,0:T(8,128)(2,1)S(1)}, f32[256,256]{1,0:T(8,128)S(1)}) custom-call(f32[1,1,256,256]{3,2,1,0:T(8,128)} %psi_hbm.1, s32[1,1,2]{2,1,0:T(1,128)} %dims_hbm.1), custom_call_target="tpu_custom_call" | custom-call | bytes 1048576 | tf_op jit(solution)/shard_map/pallas_call | solution.py:340
  1.6 0.6 %collective-permute-start = (bf16[256,256]{1,0:T(8,128)(2,1)S(1)}, bf16[256,256]{1,0:T(8,128)(2,1)S(1)}, u32[]{:S(2)}, u32[]{:S(2)}) collective-permute-start(bf16[256,256]{1,0:T(8,128)(2,1)S(1)} %get-tuple-element.19.low_ref.refs_1_), channel_id=1, source_target_pairs={{1,0},{0,1},{3,2},{2,3},{5,4},{4,5},{7,6},{6,7},{9,8},{8,9},{11,10... | collective-permute-start | bytes 393224 | tf_op jit(solution)/shard_map/ppermute | solution.py:55
  2.2 3.6 %collective-permute-start.1 = (bf16[256,256]{1,0:T(8,128)(2,1)S(1)}, bf16[256,256]{1,0:T(8,128)(2,1)S(1)}, u32[]{:S(2)}, u32[]{:S(2)}) collective-permute-start(bf16[256,256]{1,0:T(8,128)(2,1)S(1)} %get-tuple-element.19.low_ref.refs_1_), channel_id=1, source_target_pairs={{4,0},{2,1},{1,2},{7,3},{0,4},{6,5},{5,6},{3,7},{12,8},{10,9},{9,1... | collective-permute-start | bytes 393224 | tf_op jit(solution)/shard_map/ppermute | solution.py:55
  5.9 1.5 %collective-permute-start.2 = (bf16[256,256]{1,0:T(8,128)(2,1)S(1)}, bf16[256,256]{1,0:T(8,128)(2,1)S(1)}, u32[]{:S(2)}, u32[]{:S(2)}) collective-permute-start(bf16[256,256]{1,0:T(8,128)(2,1)S(1)} %get-tuple-element.19.low_ref.refs_1_), channel_id=1, source_target_pairs={{8,0},{5,1},{6,2},{11,3},{12,4},{1,5},{2,6},{15,7},{0,8},{13,9},{1... | collective-permute-start | bytes 393224 | tf_op jit(solution)/shard_map/ppermute | solution.py:55
  7.3 0.0 collective-permute-done.across_ref
  7.4 3.1 %shard_map.84 = (f32[256,256]{1,0:T(8,128)S(1)}, bf16[24,256,256]{2,1,0:T(8,128)(2,1)S(1)}, bf16[24,256,256]{2,1,0:T(8,128)(2,1)S(1)}) custom-call(bf16[1,1,30,256,256]{4,3,2,1,0:T(8,128)(2,1)} %left_hbm.1, bf16[1,1,30,256,256]{4,3,2,1,0:T(8,128)(2,1)} %right_hbm.1, bf16[256,256]{1,0:T(8,128)(2,1)S(1)} %get-tuple-element.19.low_ref.refs_1_, ...), custom_call_target="tpu_custom_call" | custom-call | flops 805306368 | bytes 8388608 | tf_op jit(solution)/shard_map/pallas_call | solution.py:366
  10.5 0.2 collective-permute-done.1.block_ref
  10.7 0.7 %shard_map.85.total_ref = f32[256,256]{1,0:T(8,128)S(1)} custom-call(bf16[24,256,256]{2,1,0:T(8,128)(2,1)S(1)} %get-tuple-element.20.left_ref, bf16[24,256,256]{2,1,0:T(8,128)(2,1)S(1)} %get-tuple-element.21.right_ref, f32[256,256]{1,0:T(8,128)S(1)} %get-tuple-element.23.total_ref, bf16[256,256]{1,0:T(8,128)(2,1)S(1)} %collective-permute-done.1.block_ref), custom_call_target="tpu_custom_call" | custom-call | flops 402653184 | tf_op jit(solution)/shard_map/pallas_call | solution.py:379
  11.4 0.0 collective-permute-done.2.refs_0_
  11.4 0.1 shard_map.86
  11.5 2.1 %collective-permute-start.3 = (bf16[256,256]{1,0:T(8,128)(2,1)S(1)}, bf16[256,256]{1,0:T(8,128)(2,1)S(1)}, u32[]{:S(2)}, u32[]{:S(2)}) collective-permute-start(bf16[256,256]{1,0:T(8,128)(2,1)S(1)} %get-tuple-element.25.low_ref), channel_id=1, source_target_pairs={{1,0},{0,1},{3,2},{2,3},{5,4},{4,5},{7,6},{6,7},{9,8},{8,9},{11,10... | collective-permute-start | bytes 393224 | tf_op jit(solution)/shard_map/ppermute | solution.py:55
  13.6 0.2 collective-permute-start.4
  13.8 1.6 %collective-permute-start.5 = (bf16[256,256]{1,0:T(8,128)(2,1)S(1)}, bf16[256,256]{1,0:T(8,128)(2,1)S(1)}, u32[]{:S(2)}, u32[]{:S(2)}) collective-permute-start(bf16[256,256]{1,0:T(8,128)(2,1)S(1)} %get-tuple-element.25.low_ref), channel_id=1, source_target_pairs={{8,0},{5,1},{6,2},{11,3},{12,4},{1,5},{2,6},{15,7},{0,8},{13,9},{1... | collective-permute-start | bytes 393224 | tf_op jit(solution)/shard_map/ppermute | solution.py:55
  15.4 0.0 collective-permute-done.3.across_ref
  15.4 1.5 %shard_map.87.total_ref = f32[256,256]{1,0:T(8,128)S(1)} custom-call(bf16[24,256,256]{2,1,0:T(8,128)(2,1)S(1)} %get-tuple-element.20.left_ref, bf16[24,256,256]{2,1,0:T(8,128)(2,1)S(1)} %get-tuple-element.21.right_ref, bf16[256,256]{1,0:T(8,128)(2,1)S(1)} %get-tuple-element.25.low_ref, bf16[256,256]{1,0:T(8,128)(2,1)S(1)} %collective-permute-done.3.across_ref), custom_call_target="tpu_custom_call" | custom-call | flops 805306368 | tf_op jit(solution)/shard_map/pallas_call | solution.py:376
  16.9 6.2 %collective-permute-done.4.block_ref = bf16[256,256]{1,0:T(8,128)(2,1)S(1)} collective-permute-done((bf16[256,256]{1,0:T(8,128)(2,1)S(1)}, bf16[256,256]{1,0:T(8,128)(2,1)S(1)}, u32[]{:S(2)}, u32[]{:S(2)}) %collective-permute-start.4) | collective-permute-done | bytes 131104 | tf_op jit(solution)/shard_map/ppermute | solution.py:55
  23.1 0.7 %shard_map.88.total_ref = f32[256,256]{1,0:T(8,128)S(1)} custom-call(bf16[24,256,256]{2,1,0:T(8,128)(2,1)S(1)} %get-tuple-element.20.left_ref, bf16[24,256,256]{2,1,0:T(8,128)(2,1)S(1)} %get-tuple-element.21.right_ref, f32[256,256]{1,0:T(8,128)S(1)} %shard_map.87.total_ref, bf16[256,256]{1,0:T(8,128)(2,1)S(1)} %collective-permute-done.4.block_ref), custom_call_target="tpu_custom_call" | custom-call | flops 402653184 | tf_op jit(solution)/shard_map/pallas_call | solution.py:379
  23.8 0.0 collective-permute-done.5.refs_0_
  23.8 0.1 shard_map.89
  23.9 0.4 collective-permute-start.6
  24.3 1.9 %collective-permute-start.13 = (bf16[512,256]{1,0:T(8,128)(2,1)S(1)}, bf16[512,256]{1,0:T(8,128)(2,1)S(1)}, u32[]{:S(2)}, u32[]{:S(2)}) collective-permute-start(bf16[512,256]{1,0:T(8,128)(2,1)S(1)} %get-tuple-element.30), channel_id=1, source_target_pairs={{0,8},{8,16},{16,24},{24,0},{1,9},{9,17},{17,25},{25,1},{2,10},{10... | collective-permute-start | bytes 786440 | tf_op jit(solution)/shard_map/ppermute | solution.py:358
  26.2 0.0 collective-permute-start.7
  26.2 1.5 %collective-permute-start.8 = (bf16[256,256]{1,0:T(8,128)(2,1)S(1)}, bf16[256,256]{1,0:T(8,128)(2,1)S(1)}, u32[]{:S(2)}, u32[]{:S(2)}) collective-permute-start(bf16[256,256]{1,0:T(8,128)(2,1)S(1)} %get-tuple-element.27.low_ref), channel_id=1, source_target_pairs={{8,0},{5,1},{6,2},{11,3},{12,4},{1,5},{2,6},{15,7},{0,8},{13,9},{1... | collective-permute-start | bytes 393224 | tf_op jit(solution)/shard_map/ppermute | solution.py:55
  27.7 0.5 %collective-permute-start.14 = (bf16[256,256]{1,0:T(8,128)(2,1)S(1)}, bf16[256,256]{1,0:T(8,128)(2,1)S(1)}, u32[]{:S(2)}, u32[]{:S(2)}) collective-permute-start(bf16[256,256]{1,0:T(8,128)(2,1)S(1)} %get-tuple-element.27.low_ref), channel_id=1, source_target_pairs={{0,8},{8,16},{16,24},{24,0},{1,9},{9,17},{17,25},{25,1},{2,10},{10... | collective-permute-start | bytes 393224 | tf_op jit(solution)/shard_map/ppermute | solution.py:362
  28.2 0.2 shard_map.90.low_ref
  28.3 0.0 collective-permute-done.6.across_ref
  28.4 1.2 %collective-permute-start.9 = (f32[8,128]{1,0:T(8,128)S(1)}, f32[8,128]{1,0:T(8,128)S(1)}, u32[]{:S(2)}, u32[]{:S(2)}) collective-permute-start(f32[8,128]{1,0:T(8,128)S(1)} %shard_map.90.low_ref), channel_id=1, source_target_pairs={{0,8},{8,16},{16,24},{24,0},{1,9},{9,17},{17,25},{25,1},{2,10},{10... | collective-permute-start | bytes 12296 | tf_op jit(solution)/shard_map/ppermute | solution.py:361
  29.5 1.5 %shard_map.91.total_ref = f32[256,256]{1,0:T(8,128)S(1)} custom-call(bf16[24,256,256]{2,1,0:T(8,128)(2,1)S(1)} %get-tuple-element.20.left_ref, bf16[24,256,256]{2,1,0:T(8,128)(2,1)S(1)} %get-tuple-element.21.right_ref, bf16[256,256]{1,0:T(8,128)(2,1)S(1)} %get-tuple-element.27.low_ref, bf16[256,256]{1,0:T(8,128)(2,1)S(1)} %collective-permute-done.6.across_ref), custom_call_target="tpu_custom_call" | custom-call | flops 805306368 | tf_op jit(solution)/shard_map/pallas_call | solution.py:376
  31.0 3.9 %collective-permute-done.7.block_ref = bf16[256,256]{1,0:T(8,128)(2,1)S(1)} collective-permute-done((bf16[256,256]{1,0:T(8,128)(2,1)S(1)}, bf16[256,256]{1,0:T(8,128)(2,1)S(1)}, u32[]{:S(2)}, u32[]{:S(2)}) %collective-permute-start.7) | collective-permute-done | bytes 131104 | tf_op jit(solution)/shard_map/ppermute | solution.py:55
  34.9 0.7 %shard_map.92.total_ref = f32[256,256]{1,0:T(8,128)S(1)} custom-call(bf16[24,256,256]{2,1,0:T(8,128)(2,1)S(1)} %get-tuple-element.20.left_ref, bf16[24,256,256]{2,1,0:T(8,128)(2,1)S(1)} %get-tuple-element.21.right_ref, f32[256,256]{1,0:T(8,128)S(1)} %shard_map.91.total_ref, bf16[256,256]{1,0:T(8,128)(2,1)S(1)} %collective-permute-done.7.block_ref), custom_call_target="tpu_custom_call" | custom-call | flops 402653184 | tf_op jit(solution)/shard_map/pallas_call | solution.py:379
  35.5 1.6 %collective-permute-done.8.refs_0_ = bf16[256,256]{1,0:T(8,128)(2,1)S(1)} collective-permute-done((bf16[256,256]{1,0:T(8,128)(2,1)S(1)}, bf16[256,256]{1,0:T(8,128)(2,1)S(1)}, u32[]{:S(2)}, u32[]{:S(2)}) %collective-permute-start.8) | collective-permute-done | bytes 131104 | tf_op jit(solution)/shard_map/ppermute | solution.py:55
  37.1 0.1 shard_map.93
  37.3 1.1 %collective-permute-done.9.prior_ref = f32[8,128]{1,0:T(8,128)S(1)} collective-permute-done((f32[8,128]{1,0:T(8,128)S(1)}, f32[8,128]{1,0:T(8,128)S(1)}, u32[]{:S(2)}, u32[]{:S(2)}) %collective-permute-start.9) | collective-permute-done | bytes 4128 | tf_op jit(solution)/shard_map/ppermute | solution.py:361
  38.3 0.0 collective-permute-start.10
  38.3 1.2 %collective-permute-done.10 = f32[24,128]{1,0:T(8,128)S(1)} collective-permute-done((f32[24,128]{1,0:T(8,128)S(1)}, f32[24,128]{1,0:T(8,128)S(1)}, u32[]{:S(2)}, u32[]{:S(2)}) %collective-permute-start.10) | collective-permute-done | bytes 12320 | tf_op jit(solution)/shard_map/ppermute | solution.py:409
  39.5 0.0 collective-permute-start.11
  39.5 3.7 %collective-permute-done.11 = f32[24,128]{1,0:T(8,128)S(1)} collective-permute-done((f32[24,128]{1,0:T(8,128)S(1)}, f32[24,128]{1,0:T(8,128)S(1)}, u32[]{:S(2)}, u32[]{:S(2)}) %collective-permute-start.11) | collective-permute-done | bytes 12320 | tf_op jit(solution)/shard_map/ppermute | solution.py:409
  43.2 0.1 collective-permute-start.12
  43.4 4.4 %collective-permute-done.12 = f32[24,128]{1,0:T(8,128)S(1)} collective-permute-done((f32[24,128]{1,0:T(8,128)S(1)}, f32[24,128]{1,0:T(8,128)S(1)}, u32[]{:S(2)}, u32[]{:S(2)}) %collective-permute-start.12) | collective-permute-done | bytes 12320 | tf_op jit(solution)/shard_map/ppermute | solution.py:409
  47.8 0.0 collective-permute-done.14.prev2_ref
  47.8 0.0 collective-permute-done.13.prev01_ref
  47.8 1.5 %shard_map.95 = (f32[1,1,256,256]{3,2,1,0:T(8,128)}, f32[1,1,256,256]{3,2,1,0:T(8,128)}, f32[1,1,256,256]{3,2,1,0:T(8,128)}, f32[1,5]{1,0:T(1,128)}, f32[1,1,256,256]{3,2,1,0:T(8,128)}) custom-call(f32[24,128]{1,0:T(8,128)S(1)} %add.11.sums_ref, f32[256,256]{1,0:T(8,128)S(1)} %get-tuple-element.18.u0_ref.refs_1_, ...), custom_call_target="tpu_custom_call" | custom-call | flops 100663296 | tf_op jit(solution)/shard_map/pallas_call | solution.py:413
  (4 shorter events, 0.0 us)
Async XLA Ops:
  1.6 5.7 %collective-permute-start = (bf16[256,256]{1,0:T(8,128)(2,1)S(1)}, bf16[256,256]{1,0:T(8,128)(2,1)S(1)}, u32[]{:S(2)}, u32[]{:S(2)}) collective-permute-start(bf16[256,256]{1,0:T(8,128)(2,1)S(1)} %get-tuple-element.19.low_ref.refs_1_), channel_id=1, source_target_pairs={{1,0},{0,1},{3,2},{2,3},{5,4},{4,5},{7,6},{6,7},{9,8},{8,9},{11,10... | collective-permute-start | bytes 393224 | tf_op jit(solution)/shard_map/ppermute | solution.py:55
  2.2 8.5 %collective-permute-start.1 = (bf16[256,256]{1,0:T(8,128)(2,1)S(1)}, bf16[256,256]{1,0:T(8,128)(2,1)S(1)}, u32[]{:S(2)}, u32[]{:S(2)}) collective-permute-start(bf16[256,256]{1,0:T(8,128)(2,1)S(1)} %get-tuple-element.19.low_ref.refs_1_), channel_id=1, source_target_pairs={{4,0},{2,1},{1,2},{7,3},{0,4},{6,5},{5,6},{3,7},{12,8},{10,9},{9,1... | collective-permute-start | bytes 393224 | tf_op jit(solution)/shard_map/ppermute | solution.py:55
  5.9 5.5 %collective-permute-start.2 = (bf16[256,256]{1,0:T(8,128)(2,1)S(1)}, bf16[256,256]{1,0:T(8,128)(2,1)S(1)}, u32[]{:S(2)}, u32[]{:S(2)}) collective-permute-start(bf16[256,256]{1,0:T(8,128)(2,1)S(1)} %get-tuple-element.19.low_ref.refs_1_), channel_id=1, source_target_pairs={{8,0},{5,1},{6,2},{11,3},{12,4},{1,5},{2,6},{15,7},{0,8},{13,9},{1... | collective-permute-start | bytes 393224 | tf_op jit(solution)/shard_map/ppermute | solution.py:55
  11.5 4.0 %collective-permute-start.3 = (bf16[256,256]{1,0:T(8,128)(2,1)S(1)}, bf16[256,256]{1,0:T(8,128)(2,1)S(1)}, u32[]{:S(2)}, u32[]{:S(2)}) collective-permute-start(bf16[256,256]{1,0:T(8,128)(2,1)S(1)} %get-tuple-element.25.low_ref), channel_id=1, source_target_pairs={{1,0},{0,1},{3,2},{2,3},{5,4},{4,5},{7,6},{6,7},{9,8},{8,9},{11,10... | collective-permute-start | bytes 393224 | tf_op jit(solution)/shard_map/ppermute | solution.py:55
  13.6 9.5 %collective-permute-start.4 = (bf16[256,256]{1,0:T(8,128)(2,1)S(1)}, bf16[256,256]{1,0:T(8,128)(2,1)S(1)}, u32[]{:S(2)}, u32[]{:S(2)}) collective-permute-start(bf16[256,256]{1,0:T(8,128)(2,1)S(1)} %get-tuple-element.25.low_ref), channel_id=1, source_target_pairs={{4,0},{2,1},{1,2},{7,3},{0,4},{6,5},{5,6},{3,7},{12,8},{10,9},{9,1... | collective-permute-start | bytes 393224 | tf_op jit(solution)/shard_map/ppermute | solution.py:55
  13.8 10.0 %collective-permute-start.5 = (bf16[256,256]{1,0:T(8,128)(2,1)S(1)}, bf16[256,256]{1,0:T(8,128)(2,1)S(1)}, u32[]{:S(2)}, u32[]{:S(2)}) collective-permute-start(bf16[256,256]{1,0:T(8,128)(2,1)S(1)} %get-tuple-element.25.low_ref), channel_id=1, source_target_pairs={{8,0},{5,1},{6,2},{11,3},{12,4},{1,5},{2,6},{15,7},{0,8},{13,9},{1... | collective-permute-start | bytes 393224 | tf_op jit(solution)/shard_map/ppermute | solution.py:55
  23.9 4.5 %collective-permute-start.6 = (bf16[256,256]{1,0:T(8,128)(2,1)S(1)}, bf16[256,256]{1,0:T(8,128)(2,1)S(1)}, u32[]{:S(2)}, u32[]{:S(2)}) collective-permute-start(bf16[256,256]{1,0:T(8,128)(2,1)S(1)} %get-tuple-element.27.low_ref), channel_id=1, source_target_pairs={{1,0},{0,1},{3,2},{2,3},{5,4},{4,5},{7,6},{6,7},{9,8},{8,9},{11,10... | collective-permute-start | bytes 393224 | tf_op jit(solution)/shard_map/ppermute | solution.py:55
  24.3 23.6 %collective-permute-start.13 = (bf16[512,256]{1,0:T(8,128)(2,1)S(1)}, bf16[512,256]{1,0:T(8,128)(2,1)S(1)}, u32[]{:S(2)}, u32[]{:S(2)}) collective-permute-start(bf16[512,256]{1,0:T(8,128)(2,1)S(1)} %get-tuple-element.30), channel_id=1, source_target_pairs={{0,8},{8,16},{16,24},{24,0},{1,9},{9,17},{17,25},{25,1},{2,10},{10... | collective-permute-start | bytes 786440 | tf_op jit(solution)/shard_map/ppermute | solution.py:358
  26.2 8.7 %collective-permute-start.7 = (bf16[256,256]{1,0:T(8,128)(2,1)S(1)}, bf16[256,256]{1,0:T(8,128)(2,1)S(1)}, u32[]{:S(2)}, u32[]{:S(2)}) collective-permute-start(bf16[256,256]{1,0:T(8,128)(2,1)S(1)} %get-tuple-element.27.low_ref), channel_id=1, source_target_pairs={{4,0},{2,1},{1,2},{7,3},{0,4},{6,5},{5,6},{3,7},{12,8},{10,9},{9,1... | collective-permute-start | bytes 393224 | tf_op jit(solution)/shard_map/ppermute | solution.py:55
  26.2 11.0 %collective-permute-start.8 = (bf16[256,256]{1,0:T(8,128)(2,1)S(1)}, bf16[256,256]{1,0:T(8,128)(2,1)S(1)}, u32[]{:S(2)}, u32[]{:S(2)}) collective-permute-start(bf16[256,256]{1,0:T(8,128)(2,1)S(1)} %get-tuple-element.27.low_ref), channel_id=1, source_target_pairs={{8,0},{5,1},{6,2},{11,3},{12,4},{1,5},{2,6},{15,7},{0,8},{13,9},{1... | collective-permute-start | bytes 393224 | tf_op jit(solution)/shard_map/ppermute | solution.py:55
  27.7 20.2 %collective-permute-start.14 = (bf16[256,256]{1,0:T(8,128)(2,1)S(1)}, bf16[256,256]{1,0:T(8,128)(2,1)S(1)}, u32[]{:S(2)}, u32[]{:S(2)}) collective-permute-start(bf16[256,256]{1,0:T(8,128)(2,1)S(1)} %get-tuple-element.27.low_ref), channel_id=1, source_target_pairs={{0,8},{8,16},{16,24},{24,0},{1,9},{9,17},{17,25},{25,1},{2,10},{10... | collective-permute-start | bytes 393224 | tf_op jit(solution)/shard_map/ppermute | solution.py:362
  28.4 10.0 %collective-permute-start.9 = (f32[8,128]{1,0:T(8,128)S(1)}, f32[8,128]{1,0:T(8,128)S(1)}, u32[]{:S(2)}, u32[]{:S(2)}) collective-permute-start(f32[8,128]{1,0:T(8,128)S(1)} %shard_map.90.low_ref), channel_id=1, source_target_pairs={{0,8},{8,16},{16,24},{24,0},{1,9},{9,17},{17,25},{25,1},{2,10},{10... | collective-permute-start | bytes 12296 | tf_op jit(solution)/shard_map/ppermute | solution.py:361
  38.3 1.2 %collective-permute-start.10 = (f32[24,128]{1,0:T(8,128)S(1)}, f32[24,128]{1,0:T(8,128)S(1)}, u32[]{:S(2)}, u32[]{:S(2)}) collective-permute-start(f32[24,128]{1,0:T(8,128)S(1)} %shard_map.94), channel_id=1, source_target_pairs={{0,1},{1,0},{2,3},{3,2},{4,5},{5,4},{6,7},{7,6},{8,9},{9,8},{10,11... | collective-permute-start | bytes 36872 | tf_op jit(solution)/shard_map/ppermute | solution.py:409
  39.5 3.7 %collective-permute-start.11 = (f32[24,128]{1,0:T(8,128)S(1)}, f32[24,128]{1,0:T(8,128)S(1)}, u32[]{:S(2)}, u32[]{:S(2)}) collective-permute-start(f32[24,128]{1,0:T(8,128)S(1)} %add.9), channel_id=1, source_target_pairs={{0,2},{1,3},{2,0},{3,1},{4,6},{5,7},{6,4},{7,5},{8,10},{9,11},{10,... | collective-permute-start | bytes 36872 | tf_op jit(solution)/shard_map/ppermute | solution.py:409
  43.2 4.6 %collective-permute-start.12 = (f32[24,128]{1,0:T(8,128)S(1)}, f32[24,128]{1,0:T(8,128)S(1)}, u32[]{:S(2)}, u32[]{:S(2)}) collective-permute-start(f32[24,128]{1,0:T(8,128)S(1)} %add.10), channel_id=1, source_target_pairs={{0,4},{1,5},{2,6},{3,7},{4,0},{5,1},{6,2},{7,3},{8,12},{9,13},{10,... | collective-permute-start | bytes 36872 | tf_op jit(solution)/shard_map/ppermute | solution.py:409

commit v4 on v3

--- a/solution.py
+++ b/solution.py
@@ -161,7 +161,7 @@
     )
 
 
-def image_into(u_ref, low_ref, ways, left_ref, right_ref, mask_ref, total_ref, blocks):
+def image_into(u_ref, low_ref, after, ways, left_ref, right_ref, mask_ref, total_ref, blocks):
     def part(k):
         return contract(slot(left_ref, 3 + k), slot(right_ref, 3 + k), blocks[k][...])
 
@@ -170,6 +170,8 @@
         u_ref[...] = u
         if low_ref is not None:
             low_ref[...] = u.astype(BF16)
+        if after is not None:
+            after(u)
 
     so_far = total_ref
     for k, way in enumerate(ways[:-1]):
@@ -198,7 +200,7 @@
         before_ref, u_ref, low_ref, pack_ref = refs[n:]
     else:
         u_ref, low_ref = refs[n:]
-    image_into(u_ref, low_ref, ways, left_ref, right_ref, mask_ref, total_ref, refs[:n])
+    image_into(u_ref, low_ref, None, ways, left_ref, right_ref, mask_ref, total_ref, refs[:n])
     if packed:
         size = low_ref.shape[0]
         pack_ref[:size] = before_ref[...]
@@ -208,11 +210,13 @@
 def last_kernel(ways, left_ref, right_ref, mask_ref, total_ref, *refs):
     n = len(ways)
     u0_ref, u1_ref, u2_ref, u_ref, dots_ref = refs[n:]
-    image_into(u_ref, None, ways, left_ref, right_ref, mask_ref, total_ref, refs[:n])
-    u = u_ref[...]
     dots_ref[...] = jnp.zeros_like(dots_ref)
-    for place, ref in enumerate((u0_ref, u1_ref, u2_ref)):
-        dots_ref[place : place + 1] = row_dot(ref[...], u)
+
+    def after(u):
+        for place, ref in enumerate((u0_ref, u1_ref, u2_ref)):
+            dots_ref[place : place + 1] = row_dot(ref[...], u)
+
+    image_into(u_ref, None, after, ways, left_ref, right_ref, mask_ref, total_ref, refs[:n])
 
 
 def gram_kernel(u0_ref, u1_ref, u2_ref, dots_ref):

time: 49.5 us -> 49.5 us (level)
  no operation moved by 1% of the time
where the time goes in v4:
time: 49.5 us; the launch traced here: 49.3 us
  waiting for transfers between devices  22.3 us (45%)
  starting transfers between devices  15.3 us (31%)
  Pallas kernels  11 us (22%)
  between operations  0.72 us (1%)
    ppermute x9, waiting for transfers between devices, permute(): return lax.ppermute(block, ('seg', 'sec'), pairs)  11.9 us
    ppermute x9, starting transfers between devices, permute(): return lax.ppermute(block, ('seg', 'sec'), pairs)  11.5 us
    ppermute x3, waiting for transfers between devices, body(): lax.ppermute(sums, 'sec', [(i, i ^ hop) for i in range(count)])  9.32 us
    pallas_call x1, Pallas kernels, body(): kernel_call(functools.partial(load_kernel, [ways['across'], ways['first']...  3.12 us
    pallas_call x2, Pallas kernels, body(): kernel_call(early_kernel, block(F32), 4, flops=2 * product)  2.94 us
    pallas_call x3, Pallas kernels, body(): kernel_call(middle_kernel, block(F32), 4, flops=product)  2.03 us
    ppermute x1, starting transfers between devices, body(): prev01 = lax.ppermute(pack, 'seg', onward)  1.89 us
    pallas_call x1, Pallas kernels, body(): kernel_call(functools.partial(end_kernel, entries), (full, full, full, ja...  1.5 us
  transfers between devices with their start and end apart: 15, of which 8 were waited for; matrix products, arithmetic and copies ran while one was open for 0% of the time, Pallas kernels for 17%

profile of v4, /device:TPU:0, one launch (start us, length us, event | category | flops | bytes accessed | tf_op | source)
XLA Modules:
  0.0 49.3 jit_solution(3587044513997153482)
XLA Ops:
  0.6 1.0 %shard_map.83 = (f32[256,256]{1,0:T(8,128)S(1)}, bf16[256,256]{1,0:T(8,128)(2,1)S(1)}, f32[256,256]{1,0:T(8,128)S(1)}) custom-call(f32[1,1,256,256]{3,2,1,0:T(8,128)} %psi_hbm.1, s32[1,1,2]{2,1,0:T(1,128)} %dims_hbm.1), custom_call_target="tpu_custom_call" | custom-call | bytes 1048576 | tf_op jit(solution)/shard_map/pallas_call | solution.py:344
  1.6 0.6 %collective-permute-start = (bf16[256,256]{1,0:T(8,128)(2,1)S(1)}, bf16[256,256]{1,0:T(8,128)(2,1)S(1)}, u32[]{:S(2)}, u32[]{:S(2)}) collective-permute-start(bf16[256,256]{1,0:T(8,128)(2,1)S(1)} %get-tuple-element.19.low_ref.refs_1_), channel_id=1, source_target_pairs={{1,0},{0,1},{3,2},{2,3},{5,4},{4,5},{7,6},{6,7},{9,8},{8,9},{11,10... | collective-permute-start | bytes 393224 | tf_op jit(solution)/shard_map/ppermute | solution.py:55
  2.2 3.6 %collective-permute-start.1 = (bf16[256,256]{1,0:T(8,128)(2,1)S(1)}, bf16[256,256]{1,0:T(8,128)(2,1)S(1)}, u32[]{:S(2)}, u32[]{:S(2)}) collective-permute-start(bf16[256,256]{1,0:T(8,128)(2,1)S(1)} %get-tuple-element.19.low_ref.refs_1_), channel_id=1, source_target_pairs={{4,0},{2,1},{1,2},{7,3},{0,4},{6,5},{5,6},{3,7},{12,8},{10,9},{9,1... | collective-permute-start | bytes 393224 | tf_op jit(solution)/shard_map/ppermute | solution.py:55
  5.9 1.5 %collective-permute-start.2 = (bf16[256,256]{1,0:T(8,128)(2,1)S(1)}, bf16[256,256]{1,0:T(8,128)(2,1)S(1)}, u32[]{:S(2)}, u32[]{:S(2)}) collective-permute-start(bf16[256,256]{1,0:T(8,128)(2,1)S(1)} %get-tuple-element.19.low_ref.refs_1_), channel_id=1, source_target_pairs={{8,0},{5,1},{6,2},{11,3},{12,4},{1,5},{2,6},{15,7},{0,8},{13,9},{1... | collective-permute-start | bytes 393224 | tf_op jit(solution)/shard_map/ppermute | solution.py:55
  7.3 0.0 collective-permute-done.across_ref
  7.4 3.1 %shard_map.84 = (f32[256,256]{1,0:T(8,128)S(1)}, bf16[24,256,256]{2,1,0:T(8,128)(2,1)S(1)}, bf16[24,256,256]{2,1,0:T(8,128)(2,1)S(1)}) custom-call(bf16[1,1,30,256,256]{4,3,2,1,0:T(8,128)(2,1)} %left_hbm.1, bf16[1,1,30,256,256]{4,3,2,1,0:T(8,128)(2,1)} %right_hbm.1, bf16[256,256]{1,0:T(8,128)(2,1)S(1)} %get-tuple-element.19.low_ref.refs_1_, ...), custom_call_target="tpu_custom_call" | custom-call | flops 805306368 | bytes 8388608 | tf_op jit(solution)/shard_map/pallas_call | solution.py:370
  10.5 0.2 collective-permute-done.1.block_ref
  10.7 0.7 %shard_map.85.total_ref = f32[256,256]{1,0:T(8,128)S(1)} custom-call(bf16[24,256,256]{2,1,0:T(8,128)(2,1)S(1)} %get-tuple-element.20.left_ref, bf16[24,256,256]{2,1,0:T(8,128)(2,1)S(1)} %get-tuple-element.21.right_ref, f32[256,256]{1,0:T(8,128)S(1)} %get-tuple-element.23.total_ref, bf16[256,256]{1,0:T(8,128)(2,1)S(1)} %collective-permute-done.1.block_ref), custom_call_target="tpu_custom_call" | custom-call | flops 402653184 | tf_op jit(solution)/shard_map/pallas_call | solution.py:383
  11.4 0.0 collective-permute-done.2.refs_0_
  11.4 0.1 shard_map.86
  11.5 2.1 %collective-permute-start.3 = (bf16[256,256]{1,0:T(8,128)(2,1)S(1)}, bf16[256,256]{1,0:T(8,128)(2,1)S(1)}, u32[]{:S(2)}, u32[]{:S(2)}) collective-permute-start(bf16[256,256]{1,0:T(8,128)(2,1)S(1)} %get-tuple-element.25.low_ref), channel_id=1, source_target_pairs={{1,0},{0,1},{3,2},{2,3},{5,4},{4,5},{7,6},{6,7},{9,8},{8,9},{11,10... | collective-permute-start | bytes 393224 | tf_op jit(solution)/shard_map/ppermute | solution.py:55
  13.6 0.2 collective-permute-start.4
  13.8 1.6 %collective-permute-start.5 = (bf16[256,256]{1,0:T(8,128)(2,1)S(1)}, bf16[256,256]{1,0:T(8,128)(2,1)S(1)}, u32[]{:S(2)}, u32[]{:S(2)}) collective-permute-start(bf16[256,256]{1,0:T(8,128)(2,1)S(1)} %get-tuple-element.25.low_ref), channel_id=1, source_target_pairs={{8,0},{5,1},{6,2},{11,3},{12,4},{1,5},{2,6},{15,7},{0,8},{13,9},{1... | collective-permute-start | bytes 393224 | tf_op jit(solution)/shard_map/ppermute | solution.py:55
  15.4 0.0 collective-permute-done.3.across_ref
  15.4 1.5 %shard_map.87.total_ref = f32[256,256]{1,0:T(8,128)S(1)} custom-call(bf16[24,256,256]{2,1,0:T(8,128)(2,1)S(1)} %get-tuple-element.20.left_ref, bf16[24,256,256]{2,1,0:T(8,128)(2,1)S(1)} %get-tuple-element.21.right_ref, bf16[256,256]{1,0:T(8,128)(2,1)S(1)} %get-tuple-element.25.low_ref, bf16[256,256]{1,0:T(8,128)(2,1)S(1)} %collective-permute-done.3.across_ref), custom_call_target="tpu_custom_call" | custom-call | flops 805306368 | tf_op jit(solution)/shard_map/pallas_call | solution.py:380
  16.9 6.2 %collective-permute-done.4.block_ref = bf16[256,256]{1,0:T(8,128)(2,1)S(1)} collective-permute-done((bf16[256,256]{1,0:T(8,128)(2,1)S(1)}, bf16[256,256]{1,0:T(8,128)(2,1)S(1)}, u32[]{:S(2)}, u32[]{:S(2)}) %collective-permute-start.4) | collective-permute-done | bytes 131104 | tf_op jit(solution)/shard_map/ppermute | solution.py:55
  23.1 0.7 %shard_map.88.total_ref = f32[256,256]{1,0:T(8,128)S(1)} custom-call(bf16[24,256,256]{2,1,0:T(8,128)(2,1)S(1)} %get-tuple-element.20.left_ref, bf16[24,256,256]{2,1,0:T(8,128)(2,1)S(1)} %get-tuple-element.21.right_ref, f32[256,256]{1,0:T(8,128)S(1)} %shard_map.87.total_ref, bf16[256,256]{1,0:T(8,128)(2,1)S(1)} %collective-permute-done.4.block_ref), custom_call_target="tpu_custom_call" | custom-call | flops 402653184 | tf_op jit(solution)/shard_map/pallas_call | solution.py:383
  23.8 0.0 collective-permute-done.5.refs_0_
  23.8 0.1 shard_map.89
  23.9 0.4 collective-permute-start.6
  24.3 1.9 %collective-permute-start.13 = (bf16[512,256]{1,0:T(8,128)(2,1)S(1)}, bf16[512,256]{1,0:T(8,128)(2,1)S(1)}, u32[]{:S(2)}, u32[]{:S(2)}) collective-permute-start(bf16[512,256]{1,0:T(8,128)(2,1)S(1)} %get-tuple-element.30), channel_id=1, source_target_pairs={{0,8},{8,16},{16,24},{24,0},{1,9},{9,17},{17,25},{25,1},{2,10},{10... | collective-permute-start | bytes 786440 | tf_op jit(solution)/shard_map/ppermute | solution.py:362
  26.2 0.0 collective-permute-start.7
  26.2 1.5 %collective-permute-start.8 = (bf16[256,256]{1,0:T(8,128)(2,1)S(1)}, bf16[256,256]{1,0:T(8,128)(2,1)S(1)}, u32[]{:S(2)}, u32[]{:S(2)}) collective-permute-start(bf16[256,256]{1,0:T(8,128)(2,1)S(1)} %get-tuple-element.27.low_ref), channel_id=1, source_target_pairs={{8,0},{5,1},{6,2},{11,3},{12,4},{1,5},{2,6},{15,7},{0,8},{13,9},{1... | collective-permute-start | bytes 393224 | tf_op jit(solution)/shard_map/ppermute | solution.py:55
  27.7 0.5 %collective-permute-start.14 = (bf16[256,256]{1,0:T(8,128)(2,1)S(1)}, bf16[256,256]{1,0:T(8,128)(2,1)S(1)}, u32[]{:S(2)}, u32[]{:S(2)}) collective-permute-start(bf16[256,256]{1,0:T(8,128)(2,1)S(1)} %get-tuple-element.27.low_ref), channel_id=1, source_target_pairs={{0,8},{8,16},{16,24},{24,0},{1,9},{9,17},{17,25},{25,1},{2,10},{10... | collective-permute-start | bytes 393224 | tf_op jit(solution)/shard_map/ppermute | solution.py:366
  28.2 0.2 shard_map.90.low_ref
  28.3 0.0 collective-permute-done.6.across_ref
  28.4 1.2 %collective-permute-start.9 = (f32[8,128]{1,0:T(8,128)S(1)}, f32[8,128]{1,0:T(8,128)S(1)}, u32[]{:S(2)}, u32[]{:S(2)}) collective-permute-start(f32[8,128]{1,0:T(8,128)S(1)} %shard_map.90.low_ref), channel_id=1, source_target_pairs={{0,8},{8,16},{16,24},{24,0},{1,9},{9,17},{17,25},{25,1},{2,10},{10... | collective-permute-start | bytes 12296 | tf_op jit(solution)/shard_map/ppermute | solution.py:365
  29.5 1.5 %shard_map.91.total_ref = f32[256,256]{1,0:T(8,128)S(1)} custom-call(bf16[24,256,256]{2,1,0:T(8,128)(2,1)S(1)} %get-tuple-element.20.left_ref, bf16[24,256,256]{2,1,0:T(8,128)(2,1)S(1)} %get-tuple-element.21.right_ref, bf16[256,256]{1,0:T(8,128)(2,1)S(1)} %get-tuple-element.27.low_ref, bf16[256,256]{1,0:T(8,128)(2,1)S(1)} %collective-permute-done.6.across_ref), custom_call_target="tpu_custom_call" | custom-call | flops 805306368 | tf_op jit(solution)/shard_map/pallas_call | solution.py:380
  31.0 3.9 %collective-permute-done.7.block_ref = bf16[256,256]{1,0:T(8,128)(2,1)S(1)} collective-permute-done((bf16[256,256]{1,0:T(8,128)(2,1)S(1)}, bf16[256,256]{1,0:T(8,128)(2,1)S(1)}, u32[]{:S(2)}, u32[]{:S(2)}) %collective-permute-start.7) | collective-permute-done | bytes 131104 | tf_op jit(solution)/shard_map/ppermute | solution.py:55
  34.9 0.7 %shard_map.92.total_ref = f32[256,256]{1,0:T(8,128)S(1)} custom-call(bf16[24,256,256]{2,1,0:T(8,128)(2,1)S(1)} %get-tuple-element.20.left_ref, bf16[24,256,256]{2,1,0:T(8,128)(2,1)S(1)} %get-tuple-element.21.right_ref, f32[256,256]{1,0:T(8,128)S(1)} %shard_map.91.total_ref, bf16[256,256]{1,0:T(8,128)(2,1)S(1)} %collective-permute-done.7.block_ref), custom_call_target="tpu_custom_call" | custom-call | flops 402653184 | tf_op jit(solution)/shard_map/pallas_call | solution.py:383
  35.5 1.6 %collective-permute-done.8.refs_0_ = bf16[256,256]{1,0:T(8,128)(2,1)S(1)} collective-permute-done((bf16[256,256]{1,0:T(8,128)(2,1)S(1)}, bf16[256,256]{1,0:T(8,128)(2,1)S(1)}, u32[]{:S(2)}, u32[]{:S(2)}) %collective-permute-start.8) | collective-permute-done | bytes 131104 | tf_op jit(solution)/shard_map/ppermute | solution.py:55
  37.1 0.1 shard_map.93
  37.3 1.1 %collective-permute-done.9.prior_ref = f32[8,128]{1,0:T(8,128)S(1)} collective-permute-done((f32[8,128]{1,0:T(8,128)S(1)}, f32[8,128]{1,0:T(8,128)S(1)}, u32[]{:S(2)}, u32[]{:S(2)}) %collective-permute-start.9) | collective-permute-done | bytes 4128 | tf_op jit(solution)/shard_map/ppermute | solution.py:365
  38.3 0.0 collective-permute-start.10
  38.3 1.2 %collective-permute-done.10 = f32[24,128]{1,0:T(8,128)S(1)} collective-permute-done((f32[24,128]{1,0:T(8,128)S(1)}, f32[24,128]{1,0:T(8,128)S(1)}, u32[]{:S(2)}, u32[]{:S(2)}) %collective-permute-start.10) | collective-permute-done | bytes 12320 | tf_op jit(solution)/shard_map/ppermute | solution.py:413
  39.5 0.0 collective-permute-start.11
  39.5 3.7 %collective-permute-done.11 = f32[24,128]{1,0:T(8,128)S(1)} collective-permute-done((f32[24,128]{1,0:T(8,128)S(1)}, f32[24,128]{1,0:T(8,128)S(1)}, u32[]{:S(2)}, u32[]{:S(2)}) %collective-permute-start.11) | collective-permute-done | bytes 12320 | tf_op jit(solution)/shard_map/ppermute | solution.py:413
  43.2 0.1 collective-permute-start.12
  43.4 4.4 %collective-permute-done.12 = f32[24,128]{1,0:T(8,128)S(1)} collective-permute-done((f32[24,128]{1,0:T(8,128)S(1)}, f32[24,128]{1,0:T(8,128)S(1)}, u32[]{:S(2)}, u32[]{:S(2)}) %collective-permute-start.12) | collective-permute-done | bytes 12320 | tf_op jit(solution)/shard_map/ppermute | solution.py:413
  47.8 0.0 collective-permute-done.14.prev2_ref
  47.8 0.0 collective-permute-done.13.prev01_ref
  47.8 1.5 %shard_map.95 = (f32[1,1,256,256]{3,2,1,0:T(8,128)}, f32[1,1,256,256]{3,2,1,0:T(8,128)}, f32[1,1,256,256]{3,2,1,0:T(8,128)}, f32[1,5]{1,0:T(1,128)}, f32[1,1,256,256]{3,2,1,0:T(8,128)}) custom-call(f32[24,128]{1,0:T(8,128)S(1)} %add.11.sums_ref, f32[256,256]{1,0:T(8,128)S(1)} %get-tuple-element.18.u0_ref.refs_1_, ...), custom_call_target="tpu_custom_call" | custom-call | flops 100663296 | tf_op jit(solution)/shard_map/pallas_call | solution.py:417
  (4 shorter events, 0.0 us)
Async XLA Ops:
  1.6 5.7 %collective-permute-start = (bf16[256,256]{1,0:T(8,128)(2,1)S(1)}, bf16[256,256]{1,0:T(8,128)(2,1)S(1)}, u32[]{:S(2)}, u32[]{:S(2)}) collective-permute-start(bf16[256,256]{1,0:T(8,128)(2,1)S(1)} %get-tuple-element.19.low_ref.refs_1_), channel_id=1, source_target_pairs={{1,0},{0,1},{3,2},{2,3},{5,4},{4,5},{7,6},{6,7},{9,8},{8,9},{11,10... | collective-permute-start | bytes 393224 | tf_op jit(solution)/shard_map/ppermute | solution.py:55
  2.2 8.5 %collective-permute-start.1 = (bf16[256,256]{1,0:T(8,128)(2,1)S(1)}, bf16[256,256]{1,0:T(8,128)(2,1)S(1)}, u32[]{:S(2)}, u32[]{:S(2)}) collective-permute-start(bf16[256,256]{1,0:T(8,128)(2,1)S(1)} %get-tuple-element.19.low_ref.refs_1_), channel_id=1, source_target_pairs={{4,0},{2,1},{1,2},{7,3},{0,4},{6,5},{5,6},{3,7},{12,8},{10,9},{9,1... | collective-permute-start | bytes 393224 | tf_op jit(solution)/shard_map/ppermute | solution.py:55
  5.9 5.5 %collective-permute-start.2 = (bf16[256,256]{1,0:T(8,128)(2,1)S(1)}, bf16[256,256]{1,0:T(8,128)(2,1)S(1)}, u32[]{:S(2)}, u32[]{:S(2)}) collective-permute-start(bf16[256,256]{1,0:T(8,128)(2,1)S(1)} %get-tuple-element.19.low_ref.refs_1_), channel_id=1, source_target_pairs={{8,0},{5,1},{6,2},{11,3},{12,4},{1,5},{2,6},{15,7},{0,8},{13,9},{1... | collective-permute-start | bytes 393224 | tf_op jit(solution)/shard_map/ppermute | solution.py:55
  11.5 4.0 %collective-permute-start.3 = (bf16[256,256]{1,0:T(8,128)(2,1)S(1)}, bf16[256,256]{1,0:T(8,128)(2,1)S(1)}, u32[]{:S(2)}, u32[]{:S(2)}) collective-permute-start(bf16[256,256]{1,0:T(8,128)(2,1)S(1)} %get-tuple-element.25.low_ref), channel_id=1, source_target_pairs={{1,0},{0,1},{3,2},{2,3},{5,4},{4,5},{7,6},{6,7},{9,8},{8,9},{11,10... | collective-permute-start | bytes 393224 | tf_op jit(solution)/shard_map/ppermute | solution.py:55
  13.6 9.5 %collective-permute-start.4 = (bf16[256,256]{1,0:T(8,128)(2,1)S(1)}, bf16[256,256]{1,0:T(8,128)(2,1)S(1)}, u32[]{:S(2)}, u32[]{:S(2)}) collective-permute-start(bf16[256,256]{1,0:T(8,128)(2,1)S(1)} %get-tuple-element.25.low_ref), channel_id=1, source_target_pairs={{4,0},{2,1},{1,2},{7,3},{0,4},{6,5},{5,6},{3,7},{12,8},{10,9},{9,1... | collective-permute-start | bytes 393224 | tf_op jit(solution)/shard_map/ppermute | solution.py:55
  13.8 10.0 %collective-permute-start.5 = (bf16[256,256]{1,0:T(8,128)(2,1)S(1)}, bf16[256,256]{1,0:T(8,128)(2,1)S(1)}, u32[]{:S(2)}, u32[]{:S(2)}) collective-permute-start(bf16[256,256]{1,0:T(8,128)(2,1)S(1)} %get-tuple-element.25.low_ref), channel_id=1, source_target_pairs={{8,0},{5,1},{6,2},{11,3},{12,4},{1,5},{2,6},{15,7},{0,8},{13,9},{1... | collective-permute-start | bytes 393224 | tf_op jit(solution)/shard_map/ppermute | solution.py:55
  23.9 4.5 %collective-permute-start.6 = (bf16[256,256]{1,0:T(8,128)(2,1)S(1)}, bf16[256,256]{1,0:T(8,128)(2,1)S(1)}, u32[]{:S(2)}, u32[]{:S(2)}) collective-permute-start(bf16[256,256]{1,0:T(8,128)(2,1)S(1)} %get-tuple-element.27.low_ref), channel_id=1, source_target_pairs={{1,0},{0,1},{3,2},{2,3},{5,4},{4,5},{7,6},{6,7},{9,8},{8,9},{11,10... | collective-permute-start | bytes 393224 | tf_op jit(solution)/shard_map/ppermute | solution.py:55
  24.3 23.6 %collective-permute-start.13 = (bf16[512,256]{1,0:T(8,128)(2,1)S(1)}, bf16[512,256]{1,0:T(8,128)(2,1)S(1)}, u32[]{:S(2)}, u32[]{:S(2)}) collective-permute-start(bf16[512,256]{1,0:T(8,128)(2,1)S(1)} %get-tuple-element.30), channel_id=1, source_target_pairs={{0,8},{8,16},{16,24},{24,0},{1,9},{9,17},{17,25},{25,1},{2,10},{10... | collective-permute-start | bytes 786440 | tf_op jit(solution)/shard_map/ppermute | solution.py:362
  26.2 8.7 %collective-permute-start.7 = (bf16[256,256]{1,0:T(8,128)(2,1)S(1)}, bf16[256,256]{1,0:T(8,128)(2,1)S(1)}, u32[]{:S(2)}, u32[]{:S(2)}) collective-permute-start(bf16[256,256]{1,0:T(8,128)(2,1)S(1)} %get-tuple-element.27.low_ref), channel_id=1, source_target_pairs={{4,0},{2,1},{1,2},{7,3},{0,4},{6,5},{5,6},{3,7},{12,8},{10,9},{9,1... | collective-permute-start | bytes 393224 | tf_op jit(solution)/shard_map/ppermute | solution.py:55
  26.2 11.0 %collective-permute-start.8 = (bf16[256,256]{1,0:T(8,128)(2,1)S(1)}, bf16[256,256]{1,0:T(8,128)(2,1)S(1)}, u32[]{:S(2)}, u32[]{:S(2)}) collective-permute-start(bf16[256,256]{1,0:T(8,128)(2,1)S(1)} %get-tuple-element.27.low_ref), channel_id=1, source_target_pairs={{8,0},{5,1},{6,2},{11,3},{12,4},{1,5},{2,6},{15,7},{0,8},{13,9},{1... | collective-permute-start | bytes 393224 | tf_op jit(solution)/shard_map/ppermute | solution.py:55
  27.7 20.2 %collective-permute-start.14 = (bf16[256,256]{1,0:T(8,128)(2,1)S(1)}, bf16[256,256]{1,0:T(8,128)(2,1)S(1)}, u32[]{:S(2)}, u32[]{:S(2)}) collective-permute-start(bf16[256,256]{1,0:T(8,128)(2,1)S(1)} %get-tuple-element.27.low_ref), channel_id=1, source_target_pairs={{0,8},{8,16},{16,24},{24,0},{1,9},{9,17},{17,25},{25,1},{2,10},{10... | collective-permute-start | bytes 393224 | tf_op jit(solution)/shard_map/ppermute | solution.py:366
  28.4 10.0 %collective-permute-start.9 = (f32[8,128]{1,0:T(8,128)S(1)}, f32[8,128]{1,0:T(8,128)S(1)}, u32[]{:S(2)}, u32[]{:S(2)}) collective-permute-start(f32[8,128]{1,0:T(8,128)S(1)} %shard_map.90.low_ref), channel_id=1, source_target_pairs={{0,8},{8,16},{16,24},{24,0},{1,9},{9,17},{17,25},{25,1},{2,10},{10... | collective-permute-start | bytes 12296 | tf_op jit(solution)/shard_map/ppermute | solution.py:365
  38.3 1.2 %collective-permute-start.10 = (f32[24,128]{1,0:T(8,128)S(1)}, f32[24,128]{1,0:T(8,128)S(1)}, u32[]{:S(2)}, u32[]{:S(2)}) collective-permute-start(f32[24,128]{1,0:T(8,128)S(1)} %shard_map.94), channel_id=1, source_target_pairs={{0,1},{1,0},{2,3},{3,2},{4,5},{5,4},{6,7},{7,6},{8,9},{9,8},{10,11... | collective-permute-start | bytes 36872 | tf_op jit(solution)/shard_map/ppermute | solution.py:413
  39.5 3.7 %collective-permute-start.11 = (f32[24,128]{1,0:T(8,128)S(1)}, f32[24,128]{1,0:T(8,128)S(1)}, u32[]{:S(2)}, u32[]{:S(2)}) collective-permute-start(f32[24,128]{1,0:T(8,128)S(1)} %add.9), channel_id=1, source_target_pairs={{0,2},{1,3},{2,0},{3,1},{4,6},{5,7},{6,4},{7,5},{8,10},{9,11},{10,... | collective-permute-start | bytes 36872 | tf_op jit(solution)/shard_map/ppermute | solution.py:413
  43.2 4.6 %collective-permute-start.12 = (f32[24,128]{1,0:T(8,128)S(1)}, f32[24,128]{1,0:T(8,128)S(1)}, u32[]{:S(2)}, u32[]{:S(2)}) collective-permute-start(f32[24,128]{1,0:T(8,128)S(1)} %add.10), channel_id=1, source_target_pairs={{0,4},{1,5},{2,6},{3,7},{4,0},{5,1},{6,2},{7,3},{8,12},{9,13},{10,... | collective-permute-start | bytes 36872 | tf_op jit(solution)/shard_map/ppermute | solution.py:413
